TPU v7x, 256 devices: a whole 4x4x8 slice. The times are simulated.
256 devices in a mesh: gx: 8 (over y, core), gy: 8 (over z), gz: 4 (over x).
Axes of the slice: x: 4, y: 4, z: 8, core: 2. Of those that a mesh axis runs over, the one named last changes fastest.
Arguments:
- rhs: float32 [32, 256, 1024], P('gz', 'gy', 'gx'), may hold values from -6 to 6
- perm_x: float32 [32, 256, 1024], P('gz', 'gy', 'gx'), may hold values from 163.84 to 1638.4
- perm_y: float32 [32, 256, 1024], P('gz', 'gy', 'gx'), may hold values from 0.001 to 0.01
- perm_z: float32 [32, 256, 1024], P('gz', 'gy', 'gx'), may hold values from 0.001 to 0.01
- storage: float32 [32, 256, 1024], P('gz', 'gy', 'gx'), may hold values from 0.002 to 0.02
- perf_cell: int32 [8, 32, 32, 8], P('gx', ('gy', 'gz')), may hold values from 0 to 32767
- perf_well: int32 [8, 32, 32, 8], P('gx', ('gy', 'gz')), may hold values from 0 to 3
- perf_index: float32 [8, 32, 32, 8], P('gx', ('gy', 'gz')), may hold values from 0.64 to 6.4
- seg_count: int32 [8, 32, 4], P('gx', ('gy', 'gz')), may hold values from 1 to 4
- bhp: float32 [8, 32, 4], P('gx', ('gy', 'gz')), may hold values from -6 to 6
Outputs:
- pressure: float32 [32, 256, 1024], P('gz', 'gy', 'gx')
- well_residual: float32 [8, 32, 4], P('gx', ('gy', 'gz'))
All inputs are finite; a program needn't handle non-finite values.
Results may differ from a plain program's by a relative error of at most 0.002.
Values sent between devices are 32-bit elements; how exact they have to be, the bound alone decides.
A program may use at most 64 MiB of HBM per device.

v0:
```python
import jax
import jax.numpy as jnp
from jax import lax
from jax.sharding import PartitionSpec as P

SEG = 4


bore_conductance = 20.0


def from_partner(x, axis, bit):
    return lax.ppermute(x, axis, [(i, i ^ 1 << bit) for i in range(lax.axis_size(axis))])


def with_halo(cells, sides, width):
    for axis, dim in sides:
        count = lax.axis_size(axis)
        ends = count - 1
        head = lax.slice_in_dim(cells, 0, width, axis=dim)
        tail = lax.slice_in_dim(cells, cells.shape[dim] - width, cells.shape[dim], axis=dim)
        cells = jnp.concatenate(
            [
                lax.ppermute(tail, axis, [(i, (i + 1) % count) for i in range(ends)]),
                cells,
                lax.ppermute(head, axis, [((i + 1) % count, i) for i in range(ends)]),
            ],
            axis=dim,
        )
    return cells


def harmonic(lower_side, upper_side):
    return 2.0 * lower_side * upper_side / (lower_side + upper_side)


def shifted(values, stride, filler, from_lower):
    filled = jnp.full(values.shape[:-1] + (stride,), filler, values.dtype)
    if from_lower:
        return jnp.concatenate([filled, values[..., :-stride]], axis=-1)
    return jnp.concatenate([values[..., stride:], filled], axis=-1)


def reduce_lines(lower_band, center, upper_band, sources):
    length = center.shape[-1]
    stride = 1
    while stride < length:
        below_center = shifted(center, stride, 1.0, True)
        above_center = shifted(center, stride, 1.0, False)
        factor_low = lower_band / below_center
        factor_high = upper_band / above_center
        new_center = (
            center
            - factor_low * shifted(upper_band, stride, 0.0, True)
            - factor_high * shifted(lower_band, stride, 0.0, False)
        )
        sources = (
            sources
            - factor_low * shifted(sources, stride, 0.0, True)
            - factor_high * shifted(sources, stride, 0.0, False)
        )
        new_lower = -factor_low * shifted(lower_band, stride, 0.0, True)
        new_upper = -factor_high * shifted(upper_band, stride, 0.0, False)
        center, lower_band, upper_band = (new_center, new_lower, new_upper)
        stride = stride * 2
    return sources / center


def join_groups(left_group, right_group):
    left_first, left_last = left_group
    right_first, right_last = right_group
    denominator = 1.0 - left_last[2] * right_first[1]
    inner_left = (
        (left_last[0] + left_last[2] * right_first[0]) / denominator,
        left_last[1] / denominator,
        left_last[2] * right_first[2] / denominator,
    )
    inner_right = (
        right_first[0] + right_first[1] * inner_left[0],
        right_first[1] * inner_left[1],
        right_first[1] * inner_left[2] + right_first[2],
    )
    merged_first = (
        left_first[0] + left_first[2] * inner_right[0],
        left_first[1] + left_first[2] * inner_right[1],
        left_first[2] * inner_right[2],
    )
    merged_last = (
        right_last[0] + right_last[1] * inner_left[0],
        right_last[1] * inner_left[1],
        right_last[1] * inner_left[2] + right_last[2],
    )
    return ((merged_first, merged_last), inner_left, inner_right)


def through_right(relation, inner_right):
    return (
        relation[0] + relation[2] * inner_right[0],
        relation[1] + relation[2] * inner_right[1],
        relation[2] * inner_right[2],
    )


def through_left(relation, inner_left):
    return (
        relation[0] + relation[1] * inner_left[0],
        relation[1] * inner_left[1],
        relation[1] * inner_left[2] + relation[2],
    )


def pick_rel(condition, when_true, when_false):
    return tuple(
        (
            jnp.where(condition, option_a, option_b)
            for option_a, option_b in zip(when_true, when_false)
        )
    )


def pack_group(block_rel):
    return jnp.stack(block_rel[0] + block_rel[1])


def unpack_group(stacked):
    return ((stacked[0], stacked[1], stacked[2]), (stacked[3], stacked[4], stacked[5]))


def boundary_swaps(block_rel):
    zero_rel = jnp.zeros_like(block_rel[0][0])
    unit_rel = jnp.ones_like(zero_rel)
    outer_low = (zero_rel, unit_rel, zero_rel)
    outer_high = (zero_rel, zero_rel, unit_rel)
    position = lax.axis_index("gx")
    for bit_level in range(lax.axis_size("gx").bit_length() - 1):
        partner = unpack_group(from_partner(pack_group(block_rel), "gx", bit_level))
        on_left = jnp.right_shift(position, bit_level) % 2 == 0
        left_group = (
            pick_rel(on_left, block_rel[0], partner[0]),
            pick_rel(on_left, block_rel[1], partner[1]),
        )
        right_group = (
            pick_rel(on_left, partner[0], block_rel[0]),
            pick_rel(on_left, partner[1], block_rel[1]),
        )
        block_rel, inner_left, inner_right = join_groups(left_group, right_group)
        outer_low = pick_rel(
            on_left, through_right(outer_low, inner_right), through_left(outer_low, inner_left)
        )
        outer_high = pick_rel(
            on_left, through_right(outer_high, inner_right), through_left(outer_high, inner_left)
        )
    return (outer_low[0], outer_high[0])


def shards(rhs, perm_x, perm_y, perm_z, storage, perf_cell, perf_well, perf_index, seg_count, bhp):
    gz_count = lax.axis_size("gz")
    group_size = lax.axis_size("gy") * gz_count
    wells_dev = seg_count.shape[-1]
    segments = SEG
    padded = with_halo(jnp.stack([perm_x, perm_y, perm_z]), (("gx", 3), ("gy", 2), ("gz", 1)), 1)
    faces_x = harmonic(padded[0, 1:-1, 1:-1, :-1], padded[0, 1:-1, 1:-1, 1:])
    faces_y = harmonic(padded[1, 1:-1, :-1, 1:-1], padded[1, 1:-1, 1:, 1:-1])
    faces_z = harmonic(padded[2, :-1, 1:-1, 1:-1], padded[2, 1:, 1:-1, 1:-1])
    x_lower = faces_x[..., :-1]
    x_upper = faces_x[..., 1:]
    y_lower = faces_y[:, :-1, :]
    y_upper = faces_y[:, 1:, :]
    z_lower = faces_z[:-1]
    z_upper = faces_z[1:]
    center = storage + x_lower + x_upper + y_lower + y_upper + z_lower + z_upper
    zero_column = jnp.zeros_like(center[..., :1])
    lower_band = jnp.concatenate([zero_column, -x_lower[..., 1:]], axis=-1)
    upper_band = jnp.concatenate([-x_upper[..., :-1], zero_column], axis=-1)
    zero_rest = jnp.zeros_like(center[..., 1:])
    spike_low = jnp.concatenate([x_lower[..., :1], zero_rest], axis=-1)
    spike_high = jnp.concatenate([zero_rest, x_upper[..., -1:]], axis=-1)
    cells_flat = perf_cell[0, 0].reshape(-1)
    local_weight = perf_index[0, 0]
    source_layer = (jnp.arange(group_size) % gz_count)[:, None]
    bore_seg = jnp.repeat(bhp[0, 0], segments)
    counts = seg_count[0, 0]
    well_slots = jnp.arange(wells_dev)
    seg_slots = jnp.arange(wells_dev * segments)
    arrived_well = lax.all_to_all(
        perf_well[0, 0], ("gy", "gz"), split_axis=0, concat_axis=0, tiled=True
    )
    arrived_weight = lax.all_to_all(
        local_weight, ("gy", "gz"), split_axis=0, concat_axis=0, tiled=True
    )
    owned = arrived_well[..., None] == well_slots
    arrived_count = jnp.sum(jnp.where(owned, counts, 0), axis=-1)
    slot_index = arrived_well * segments + source_layer * arrived_count // gz_count
    selector = (slot_index[..., None] == seg_slots).astype(jnp.float32)
    seg_weight = jnp.sum(selector * arrived_weight[..., None], axis=(0, 1))

    def send_pressure(perforated):
        arrived = lax.all_to_all(perforated, ("gy", "gz"), split_axis=0, concat_axis=0, tiled=True)
        return jnp.sum(selector * (arrived_weight * arrived)[..., None], axis=(0, 1))

    def return_pressure(seg_pressure):
        per_slot = jnp.sum(selector * seg_pressure, axis=-1)
        return lax.all_to_all(per_slot, ("gy", "gz"), split_axis=0, concat_axis=0, tiled=True)

    denominator = seg_weight + bore_conductance

    def scatter_cells(flow_terms):
        summed = jnp.zeros((rhs.size,), jnp.float32).at[cells_flat].add(flow_terms.reshape(-1))
        return summed.reshape(rhs.shape)

    def perforated_of(pressure_field):
        return pressure_field.reshape(-1)[cells_flat].reshape(local_weight.shape)

    def boundaries(line_values, spike_left, spike_right):
        block_rel = (
            (line_values[..., 0], spike_left[..., 0], spike_right[..., 0]),
            (line_values[..., -1], spike_left[..., -1], spike_right[..., -1]),
        )
        return boundary_swaps(block_rel)

    start_segments = bore_conductance * bore_seg / denominator
    back_first = return_pressure(start_segments)
    first_source = rhs - scatter_cells(local_weight * (0.0 - back_first))
    solved = reduce_lines(
        lower_band, center, upper_band, jnp.stack([first_source, spike_low, spike_high])
    )
    line_values = solved[0]
    spike_left = solved[1]
    spike_right = solved[2]
    low_value, high_value = boundaries(line_values, spike_left, spike_right)
    first_pass = (
        line_values + spike_left * low_value[..., None] + spike_right * high_value[..., None]
    )
    extended = with_halo(first_pass, (("gx", 2), ("gy", 1), ("gz", 0)), 1)
    beside = x_lower * extended[1:-1, 1:-1, :-2] + x_upper * extended[1:-1, 1:-1, 2:]
    beside = beside + y_lower * extended[1:-1, :-2, 1:-1] + y_upper * extended[1:-1, 2:, 1:-1]
    beside = beside + z_lower * extended[:-2, 1:-1, 1:-1] + z_upper * extended[2:, 1:-1, 1:-1]
    applied = center * first_pass - beside
    perforated = perforated_of(first_pass)
    seg_pressure = (send_pressure(perforated) + bore_conductance * bore_seg) / denominator
    back_second = return_pressure(seg_pressure)
    second_source = rhs - applied - scatter_cells(local_weight * (perforated - back_second))
    second_values = reduce_lines(lower_band, center, upper_band, second_source[None])[0]
    low_value, high_value = boundaries(second_values, spike_left, spike_right)
    pressure = first_pass + (
        second_values + spike_left * low_value[..., None] + spike_right * high_value[..., None]
    )
    final_segments = (
        send_pressure(perforated_of(pressure)) + bore_conductance * bore_seg
    ) / denominator
    well_residual = jnp.sum(
        (final_segments - bore_seg).reshape(wells_dev, segments), axis=-1
    ).reshape(1, 1, wells_dev)
    return (pressure, well_residual)


def solution(mesh):
    return jax.shard_map(
        shards,
        mesh=mesh,
        in_specs=(
            P("gz", "gy", "gx"),
            P("gz", "gy", "gx"),
            P("gz", "gy", "gx"),
            P("gz", "gy", "gx"),
            P("gz", "gy", "gx"),
            P("gx", ("gy", "gz"), None, None),
            P("gx", ("gy", "gz"), None, None),
            P("gx", ("gy", "gz"), None, None),
            P("gx", ("gy", "gz"), None),
            P("gx", ("gy", "gz"), None),
        ),
        out_specs=(P("gz", "gy", "gx"), P("gx", ("gy", "gz"), None)),
        check_vma=False,
    )
```

profile of v0, /device:TPU:1, one launch (start us, length us, event | category | flops | bytes accessed | tf_op | source)
XLA Modules:
  0.0 196.3 jit_solution(1434304635941485814)
XLA Ops:
  0.6 1.1 pad_maximum_fusion
  2.0 4.7 %collective-permute-start = (f32[3,8,32,1]{3,2,1,0:T(8,128)S(1)}, f32[3,8,32,1]{3,2,1,0:T(8,128)S(1)}, u32[]{:S(2)}, u32[]{:S(2)}) collective-permute-start(f32[3,8,32,1]{3,2,1,0:T(8,128)S(1)} %get-tuple-element.101), channel_id=1, source_target_pairs={{0,32},{32,64},{64,96},{96,128},{128,160},{160,192},{192,224},{1,3... | collective-permute-start | bytes 9224 | tf_op jit(solution)/shard_map/ppermute | solution.py:24
  6.7 1.9 collective-permute-start.1
  9.3 11.0 %all-to-all-start.1 = ((f32[32,1,8]{2,1,0:T(1,128)}), f32[32,1,8]{2,1,0:T(1,128)S(1)}, u32[]{:S(2)}, u32[]{:S(2)}) async-start(f32[32,1,8]{2,1,0:T(1,128)} %bitcast.5), calls=%async_computation.1 | async-start | bytes 32768 | tf_op jit(solution)/shard_map/all_to_all | solution.py:188
  21.3 7.6 %all-to-all-done.1 = f32[32,1,8]{2,1,0:T(1,128)S(1)} async-done(((f32[32,1,8]{2,1,0:T(1,128)}), f32[32,1,8]{2,1,0:T(1,128)S(1)}, u32[]{:S(2)}, u32[]{:S(2)}) %all-to-all-start.1) | async-done | bytes 1056 | tf_op jit(solution)/shard_map/all_to_all | solution.py:188
  28.9 3.9 %all-to-all-start = ((s32[32,1,8]{2,1,0:T(1,128)}), s32[32,1,8]{2,1,0:T(1,128)S(1)}, u32[]{:S(2)}, u32[]{:S(2)}) async-start(s32[32,1,8]{2,1,0:T(1,128)} %bitcast.1), calls=%async_computation | async-start | bytes 32768 | tf_op jit(solution)/shard_map/all_to_all | solution.py:185
  32.8 0.8 squeeze.156
  33.8 7.6 %all-to-all-done = s32[32,1,8]{2,1,0:T(1,128)S(1)} async-done(((s32[32,1,8]{2,1,0:T(1,128)}), s32[32,1,8]{2,1,0:T(1,128)S(1)}, u32[]{:S(2)}, u32[]{:S(2)}) %all-to-all-start) | async-done | bytes 1056 | tf_op jit(solution)/shard_map/all_to_all | solution.py:185
  42.9 3.8 %all-to-all-start.2 = ((f32[32,1,8]{2,1,0:T(1,128)}), f32[32,1,8]{2,1,0:T(1,128)S(1)}, u32[]{:S(2)}, u32[]{:S(2)}) async-start(f32[32,1,8]{2,1,0:T(1,128)} %copy.2690), calls=%async_computation.2 | async-start | bytes 32768 | tf_op jit(solution)/shard_map/all_to_all | solution.py:203
  47.4 3.2 %collective-permute-start.2 = (f32[3,8,1,130]{3,2,1,0:T(1,128)S(1)}, f32[3,8,1,130]{3,2,1,0:T(1,128)S(1)}, u32[]{:S(2)}, u32[]{:S(2)}) collective-permute-start(f32[3,8,1,130]{3,2,1,0:T(1,128)S(1)} %get-tuple-element.75), channel_id=1, source_target_pairs={{0,4},{4,8},{8,12},{12,16},{16,20},{20,24},{24,28},{1,5},{5,9},{9,... | collective-permute-start | bytes 37448 | tf_op jit(solution)/shard_map/ppermute | solution.py:24
  50.5 1.3 collective-permute-start.3
  51.8 3.5 %all-to-all-done.2 = f32[32,1,8]{2,1,0:T(1,128)S(1)} async-done(((f32[32,1,8]{2,1,0:T(1,128)}), f32[32,1,8]{2,1,0:T(1,128)S(1)}, u32[]{:S(2)}, u32[]{:S(2)}) %all-to-all-start.2) | async-done | bytes 1056 | tf_op jit(solution)/shard_map/all_to_all | solution.py:203
  55.4 2.0 %scatter_custom_fusion = f32[32768]{0:T(1024)S(1)} fusion(s32[256]{0:T(256)S(1)} %bitcast.433, f32[256]{0:T(256)S(1)} %mul.1137, f32[]{:T(128)} %constant.46.clone.1), kind=kCustom, calls=%fused_computation.277 | custom fusion | flops 256 | bytes 131076 | tf_op jit(solution)/shard_map/scatter-add | solution.py:208
  57.7 2.2 %collective-permute-start.4 = (f32[3,1,34,130]{3,2,1,0:T(8,128)S(1)}, f32[3,1,34,130]{3,2,1,0:T(8,128)S(1)}, u32[]{:S(2)}, u32[]{:S(2)}) collective-permute-start(f32[3,1,34,130]{3,2,1,0:T(8,128)S(1)} %get-tuple-element.73), channel_id=1, source_target_pairs={{0,1},{1,2},{2,3},{4,5},{5,6},{6,7},{8,9},{9,10},{10,11},{12,13},{... | collective-permute-start | bytes 159128 | tf_op jit(solution)/shard_map/ppermute | solution.py:24
  59.9 1.3 collective-permute-start.5
  61.8 3.8 %collective-permute-done.5 = f32[3,1,34,130]{3,2,1,0:T(8,128)S(1)} collective-permute-done((f32[3,1,34,130]{3,2,1,0:T(8,128)S(1)}, f32[3,1,34,130]{3,2,1,0:T(8,128)S(1)}, u32[]{:S(2)}, u32[]{:S(2)}) %collective-permute-start.5) | collective-permute-done | bytes 53072 | tf_op jit(solution)/shard_map/ppermute | solution.py:26
  74.4 3.1 %collective-permute-start.6 = (f32[6,8,32]{2,1,0:T(8,128)S(1)}, f32[6,8,32]{2,1,0:T(8,128)S(1)}, u32[]{:S(2)}, u32[]{:S(2)}) collective-permute-start(f32[6,8,32]{2,1,0:T(8,128)S(1)} %constant_dynamic-update-slice_fusion), channel_id=1, source_target_pairs={{0,32},{32,0},{64,96},{96,64},{128,160},{160,128},{192,224},{224,1... | collective-permute-start | bytes 18440 | tf_op jit(solution)/shard_map/ppermute | solution.py:13
  77.5 0.8 collective-permute-done.6
  78.5 3.9 %collective-permute-start.7 = (f32[6,8,32]{2,1,0:T(8,128)S(1)}, f32[6,8,32]{2,1,0:T(8,128)S(1)}, u32[]{:S(2)}, u32[]{:S(2)}) collective-permute-start(f32[6,8,32]{2,1,0:T(8,128)S(1)} %get-tuple-element.32), channel_id=1, source_target_pairs={{0,64},{32,96},{64,0},{96,32},{128,192},{160,224},{192,128},{224,1... | collective-permute-start | bytes 18440 | tf_op jit(solution)/shard_map/ppermute | solution.py:13
  82.4 1.2 collective-permute-done.7
  87.2 3.1 %collective-permute-start.8 = (f32[6,8,32]{2,1,0:T(8,128)}, f32[6,8,32]{2,1,0:T(8,128)}, u32[]{:S(2)}, u32[]{:S(2)}) collective-permute-start(f32[6,8,32]{2,1,0:T(8,128)} %constant_dynamic-update-slice_fusion.12), channel_id=1, source_target_pairs={{0,128},{32,160},{64,192},{96,224},{128,0},{160,32},{192,64},{224,... | collective-permute-start | bytes 18440 | tf_op jit(solution)/shard_map/ppermute | solution.py:13
  92.3 0.8 copy.2700
  95.4 0.8 copy.2706
  97.0 0.8 copy.2712
  100.9 0.8 copy.2718
  101.7 2.2 %select_reduce_fusion.3 = f32[8,32]{1,0:T(8,128)S(1)} fusion(f32[8,32,1]{2,1,0:T(8,128)} %copy.2718, f32[8,32,1]{2,1,0:T(8,128)} %copy.2706, f32[8,32,1]{2,1,0:T(8,128)} %copy.2716, f32[8,32,1]{2,1,0:T(8,128)} %copy.2712, f32[8,32,1]{2,1,0:T(8,128)} %copy.2704, f32[8,32,1]{2,1,0:T(8,128)} %copy.2713, f32[8,32,1]{2,1,0:T(8,128)} %copy.2701, ...), kind=kLoop, calls=%fused_computation.146 | loop fusion | flops 26624 | bytes 23555 | tf_op jit(solution)/shard_map/jit(_where)/select_n | solution.py:115
  105.8 3.7 %collective-permute-start.10 = (f32[8,32,1]{2,1,0:T(8,128)}, f32[8,32,1]{2,1,0:T(8,128)}, u32[]{:S(2)}, u32[]{:S(2)}) collective-permute-start(f32[8,32,1]{2,1,0:T(8,128)} %get-tuple-element.120), channel_id=1, source_target_pairs={{32,0},{64,32},{96,64},{128,96},{160,128},{192,160},{224,192},{33,... | collective-permute-start | bytes 3080 | tf_op jit(solution)/shard_map/ppermute | solution.py:26
  109.4 2.2 %collective-permute-start.9 = (f32[8,32,1]{2,1,0:T(8,128)}, f32[8,32,1]{2,1,0:T(8,128)}, u32[]{:S(2)}, u32[]{:S(2)}) collective-permute-start(f32[8,32,1]{2,1,0:T(8,128)} %get-tuple-element.119), channel_id=1, source_target_pairs={{0,32},{32,64},{64,96},{96,128},{128,160},{160,192},{192,224},{1,3... | collective-permute-start | bytes 3080 | tf_op jit(solution)/shard_map/ppermute | solution.py:24
  111.9 1.7 gather_fusion
  114.4 8.3 %all-to-all-start.3 = ((f32[32,1,8]{2,1,0:T(1,128)}), f32[32,1,8]{2,1,0:T(1,128)S(1)}, u32[]{:S(2)}, u32[]{:S(2)}) async-start(f32[32,1,8]{2,1,0:T(1,128)} %bitcast.45), calls=%async_computation.3 | async-start | bytes 32768 | tf_op jit(solution)/shard_map/all_to_all | solution.py:198
  122.7 1.5 pad_maximum_fusion.55
  124.2 3.1 %collective-permute-start.11 = (f32[8,1,130]{2,1,0:T(1,128)}, f32[8,1,130]{2,1,0:T(1,128)S(1)}, u32[]{:S(2)}, u32[]{:S(2)}) collective-permute-start(f32[8,1,130]{2,1,0:T(1,128)} %get-tuple-element.79), channel_id=1, source_target_pairs={{0,4},{4,8},{8,12},{12,16},{16,20},{20,24},{24,28},{1,5},{5,9},{9,... | collective-permute-start | bytes 12488 | tf_op jit(solution)/shard_map/ppermute | solution.py:24
  127.3 1.3 collective-permute-start.12
  128.6 2.4 %all-to-all-done.3 = f32[32,1,8]{2,1,0:T(1,128)S(1)} async-done(((f32[32,1,8]{2,1,0:T(1,128)}), f32[32,1,8]{2,1,0:T(1,128)S(1)}, u32[]{:S(2)}, u32[]{:S(2)}) %all-to-all-start.3) | async-done | bytes 1056 | tf_op jit(solution)/shard_map/all_to_all | solution.py:198
  132.1 17.2 %all_to_all.66 = f32[32,1,8]{2,1,0:T(1,128)S(1)} all-to-all(f32[32,1,8]{2,1,0:T(1,128)S(1)} %copy.2721), channel_id=1, replica_groups=mesh['gx'=8,'gy'=8,'gz'=4] {'gy','gz'}, dimensions={0} | all-to-all | bytes 2048 | tf_op jit(solution)/shard_map/all_to_all | solution.py:203
  151.3 1.5 pad_maximum_fusion.47
  152.8 2.8 %collective-permute-start.13 = (f32[1,34,130]{2,1,0:T(8,128)}, f32[1,34,130]{2,1,0:T(8,128)}, u32[]{:S(2)}, u32[]{:S(2)}) collective-permute-start(f32[1,34,130]{2,1,0:T(8,128)} %get-tuple-element.77), channel_id=1, source_target_pairs={{0,1},{1,2},{2,3},{4,5},{5,6},{6,7},{8,9},{9,10},{10,11},{12,13},{... | collective-permute-start | bytes 53048 | tf_op jit(solution)/shard_map/ppermute | solution.py:24
  155.6 1.3 collective-permute-start.14
  157.5 2.7 %scatter_custom_fusion.1 = f32[32768]{0:T(1024)} fusion(s32[256]{0:T(256)} %bitcast.435, f32[256]{0:T(256)} %subtract_multiply_fusion, f32[]{:T(128)} %constant.46.clone.1), kind=kCustom, calls=%fused_computation.275 | custom fusion | flops 256 | bytes 131584 | tf_op jit(solution)/shard_map/scatter-add | solution.py:208
  160.4 1.7 fusion.25
  164.9 4.9 %collective-permute-start.15 = (f32[6,8,32]{2,1,0:T(8,128)S(1)}, f32[6,8,32]{2,1,0:T(8,128)S(1)}, u32[]{:S(2)}, u32[]{:S(2)}) collective-permute-start(f32[6,8,32]{2,1,0:T(8,128)S(1)} %constant_dynamic-update-slice_fusion.18), channel_id=1, source_target_pairs={{0,32},{32,0},{64,96},{96,64},{128,160},{160,128},{192,224},{224,1... | collective-permute-start | bytes 18440 | tf_op jit(solution)/shard_map/ppermute | solution.py:13
  169.9 0.8 collective-permute-done.15
  170.9 2.7 %collective-permute-done.16 = f32[6,8,32]{2,1,0:T(8,128)S(1)} collective-permute-done((f32[6,8,32]{2,1,0:T(8,128)S(1)}, f32[6,8,32]{2,1,0:T(8,128)S(1)}, u32[]{:S(2)}, u32[]{:S(2)}) %collective-permute-start.16) | collective-permute-done | bytes 6176 | tf_op jit(solution)/shard_map/ppermute | solution.py:13
  175.9 2.0 %collective-permute-done.17 = f32[6,8,32]{2,1,0:T(8,128)S(1)} collective-permute-done((f32[6,8,32]{2,1,0:T(8,128)S(1)}, f32[6,8,32]{2,1,0:T(8,128)S(1)}, u32[]{:S(2)}, u32[]{:S(2)}) %collective-permute-start.17) | collective-permute-done | bytes 6176 | tf_op jit(solution)/shard_map/ppermute | solution.py:13
  180.1 1.9 gather_fusion.1
  182.7 4.0 %all-to-all-start.5 = ((f32[32,1,8]{2,1,0:T(1,128)}), f32[32,1,8]{2,1,0:T(1,128)S(1)}, u32[]{:S(2)}, u32[]{:S(2)}) async-start(f32[32,1,8]{2,1,0:T(1,128)} %bitcast.85), calls=%async_computation.5 | async-start | bytes 32768 | tf_op jit(solution)/shard_map/all_to_all | solution.py:198
  186.7 0.9 add_add_fusion.1
  187.6 7.7 %all-to-all-done.5 = f32[32,1,8]{2,1,0:T(1,128)S(1)} async-done(((f32[32,1,8]{2,1,0:T(1,128)}), f32[32,1,8]{2,1,0:T(1,128)S(1)}, u32[]{:S(2)}, u32[]{:S(2)}) %all-to-all-start.5) | async-done | bytes 1056 | tf_op jit(solution)/shard_map/all_to_all | solution.py:198
  (301 shorter events, 40.5 us)
Async XLA Ops:
  1.7 6.9 %copy-start.33 = (f32[1,1,32,8]{2,3,1,0:T(8,128)S(1)}, f32[1,1,32,8]{2,3,1,0:T(8,128)}, u32[]{:S(2)}) copy-start(f32[1,1,32,8]{2,3,1,0:T(8,128)} %param.17) | copy-start | bytes 3076
  1.7 18.7 %copy-start.34 = (s32[1,1,32,8]{2,3,1,0:T(8,128)S(1)}, s32[1,1,32,8]{2,3,1,0:T(8,128)}, u32[]{:S(2)}) copy-start(s32[1,1,32,8]{2,3,1,0:T(8,128)} %param.15) | copy-start | bytes 3076
  1.7 18.8 %copy-start.43 = (f32[1,1,4]{2,1,0:T(1,128)S(1)}, f32[1,1,4]{2,1,0:T(1,128)}, u32[]{:S(2)}) copy-start(f32[1,1,4]{2,1,0:T(1,128)} %param.19) | copy-start | bytes 52
  1.7 18.9 %copy-start.35 = (s32[1,1,32,8]{2,3,1,0:T(8,128)S(1)}, s32[1,1,32,8]{2,3,1,0:T(8,128)}, u32[]{:S(2)}) copy-start(s32[1,1,32,8]{2,3,1,0:T(8,128)} %param.16) | copy-start | bytes 3076
  1.7 39.7 %copy-start.42 = (s32[1,1,4]{2,1,0:T(1,128)S(1)}, s32[1,1,4]{2,1,0:T(1,128)}, u32[]{:S(2)}) copy-start(s32[1,1,4]{2,1,0:T(1,128)} %param.18) | copy-start | bytes 52
  1.8 45.0 %copy-start.2 = (f32[8,32,128]{2,1,0:T(8,128)S(1)}, f32[8,32,128]{2,1,0:T(8,128)}, u32[]{:S(2)}) copy-start(f32[8,32,128]{2,1,0:T(8,128)} %param.11) | copy-start | bytes 393220
  1.9 44.9 %copy-start = (f32[8,32,128]{2,1,0:T(8,128)S(1)}, f32[8,32,128]{2,1,0:T(8,128)}, u32[]{:S(2)}) copy-start(f32[8,32,128]{2,1,0:T(8,128)} %param.13) | copy-start | bytes 393220
  2.0 44.9 %copy-start.1 = (f32[8,32,128]{2,1,0:T(8,128)S(1)}, f32[8,32,128]{2,1,0:T(8,128)}, u32[]{:S(2)}) copy-start(f32[8,32,128]{2,1,0:T(8,128)} %param.12) | copy-start | bytes 393220
  2.0 44.8 %collective-permute-start = (f32[3,8,32,1]{3,2,1,0:T(8,128)S(1)}, f32[3,8,32,1]{3,2,1,0:T(8,128)S(1)}, u32[]{:S(2)}, u32[]{:S(2)}) collective-permute-start(f32[3,8,32,1]{3,2,1,0:T(8,128)S(1)} %get-tuple-element.101), channel_id=1, source_target_pairs={{0,32},{32,64},{64,96},{96,128},{128,160},{160,192},{192,224},{1,3... | collective-permute-start | bytes 9224 | tf_op jit(solution)/shard_map/ppermute | solution.py:24
  6.7 40.1 %collective-permute-start.1 = (f32[3,8,32,1]{3,2,1,0:T(8,128)S(1)}, f32[3,8,32,1]{3,2,1,0:T(8,128)S(1)}, u32[]{:S(2)}, u32[]{:S(2)}) collective-permute-start(f32[3,8,32,1]{3,2,1,0:T(8,128)S(1)} %get-tuple-element.102), channel_id=1, source_target_pairs={{32,0},{64,32},{96,64},{128,96},{160,128},{192,160},{224,192},{33,... | collective-permute-start | bytes 9224 | tf_op jit(solution)/shard_map/ppermute | solution.py:26
  9.3 19.6 %all-to-all-start.1 = ((f32[32,1,8]{2,1,0:T(1,128)}), f32[32,1,8]{2,1,0:T(1,128)S(1)}, u32[]{:S(2)}, u32[]{:S(2)}) async-start(f32[32,1,8]{2,1,0:T(1,128)} %bitcast.5), calls=%async_computation.1 | async-start | bytes 32768 | tf_op jit(solution)/shard_map/all_to_all | solution.py:188
  20.6 69.7 %copy-start.36 = (s32[256,1]{0,1:T(1,128)}, s32[256,1]{0,1:T(1,128)S(1)}, u32[]{:S(2)}) copy-start(s32[256,1]{0,1:T(1,128)S(1)} %compare_select_fusion) | copy-start | bytes 3076
  20.6 26.4 %copy-start.39 = (f32[4]{0:T(128)}, f32[4]{0:T(128)S(1)}, u32[]{:S(2)}) copy-start(f32[4]{0:T(128)S(1)} %broadcast_multiply_fusion) | copy-start | bytes 52
  28.9 12.5 %all-to-all-start = ((s32[32,1,8]{2,1,0:T(1,128)}), s32[32,1,8]{2,1,0:T(1,128)S(1)}, u32[]{:S(2)}, u32[]{:S(2)}) async-start(s32[32,1,8]{2,1,0:T(1,128)} %bitcast.1), calls=%async_computation | async-start | bytes 32768 | tf_op jit(solution)/shard_map/all_to_all | solution.py:185
  33.7 13.3 %copy-start.30 = (f32[16]{0:T(128)}, f32[16]{0:T(128)S(1)}, u32[]{:S(2)}) copy-start(f32[16]{0:T(128)S(1)} %mul.1131) | copy-start | bytes 196
  42.9 12.4 %all-to-all-start.2 = ((f32[32,1,8]{2,1,0:T(1,128)}), f32[32,1,8]{2,1,0:T(1,128)S(1)}, u32[]{:S(2)}, u32[]{:S(2)}) async-start(f32[32,1,8]{2,1,0:T(1,128)} %copy.2690), calls=%async_computation.2 | async-start | bytes 32768 | tf_op jit(solution)/shard_map/all_to_all | solution.py:203
  47.3 10.1 %copy-start.24 = (f32[8,32,128]{2,1,0:T(8,128)S(1)}, f32[8,32,128]{2,1,0:T(8,128)}, u32[]{:S(2)}) copy-start(f32[8,32,128]{2,1,0:T(8,128)} %param.10) | copy-start | bytes 393220
  47.4 10.2 %collective-permute-start.2 = (f32[3,8,1,130]{3,2,1,0:T(1,128)S(1)}, f32[3,8,1,130]{3,2,1,0:T(1,128)S(1)}, u32[]{:S(2)}, u32[]{:S(2)}) collective-permute-start(f32[3,8,1,130]{3,2,1,0:T(1,128)S(1)} %get-tuple-element.75), channel_id=1, source_target_pairs={{0,4},{4,8},{8,12},{12,16},{16,20},{20,24},{24,28},{1,5},{5,9},{9,... | collective-permute-start | bytes 37448 | tf_op jit(solution)/shard_map/ppermute | solution.py:24
  50.5 7.0 %collective-permute-start.3 = (f32[3,8,1,130]{3,2,1,0:T(1,128)S(1)}, f32[3,8,1,130]{3,2,1,0:T(1,128)S(1)}, u32[]{:S(2)}, u32[]{:S(2)}) collective-permute-start(f32[3,8,1,130]{3,2,1,0:T(1,128)S(1)} %get-tuple-element.76), channel_id=1, source_target_pairs={{4,0},{8,4},{12,8},{16,12},{20,16},{24,20},{28,24},{5,1},{9,5},{13... | collective-permute-start | bytes 37448 | tf_op jit(solution)/shard_map/ppermute | solution.py:26
  57.7 4.1 %collective-permute-start.4 = (f32[3,1,34,130]{3,2,1,0:T(8,128)S(1)}, f32[3,1,34,130]{3,2,1,0:T(8,128)S(1)}, u32[]{:S(2)}, u32[]{:S(2)}) collective-permute-start(f32[3,1,34,130]{3,2,1,0:T(8,128)S(1)} %get-tuple-element.73), channel_id=1, source_target_pairs={{0,1},{1,2},{2,3},{4,5},{5,6},{6,7},{8,9},{9,10},{10,11},{12,13},{... | collective-permute-start | bytes 159128 | tf_op jit(solution)/shard_map/ppermute | solution.py:24
  59.9 5.6 %collective-permute-start.5 = (f32[3,1,34,130]{3,2,1,0:T(8,128)S(1)}, f32[3,1,34,130]{3,2,1,0:T(8,128)S(1)}, u32[]{:S(2)}, u32[]{:S(2)}) collective-permute-start(f32[3,1,34,130]{3,2,1,0:T(8,128)S(1)} %get-tuple-element.74), channel_id=1, source_target_pairs={{1,0},{2,1},{3,2},{5,4},{6,5},{7,6},{9,8},{10,9},{11,10},{13,12},{... | collective-permute-start | bytes 159128 | tf_op jit(solution)/shard_map/ppermute | solution.py:26
  61.4 4.3 %copy-start.26 = (f32[8,32,128]{2,1,0:T(8,128)S(1)}, f32[8,32,128]{2,1,0:T(8,128)}, u32[]{:S(2)}) copy-start(f32[8,32,128]{2,1,0:T(8,128)} %param.14) | copy-start | bytes 393220
  61.4 4.3 %copy-start.41 = (pred[128]{0:T(512)(128)(4,1)S(1)}, pred[128]{0:T(512)(128)(4,1)}, u32[]{:S(2)}) copy-start(pred[128]{0:T(512)(128)(4,1)} %constant.109.clone.1) | copy-start | bytes 388
  74.4 3.9 %collective-permute-start.6 = (f32[6,8,32]{2,1,0:T(8,128)S(1)}, f32[6,8,32]{2,1,0:T(8,128)S(1)}, u32[]{:S(2)}, u32[]{:S(2)}) collective-permute-start(f32[6,8,32]{2,1,0:T(8,128)S(1)} %constant_dynamic-update-slice_fusion), channel_id=1, source_target_pairs={{0,32},{32,0},{64,96},{96,64},{128,160},{160,128},{192,224},{224,1... | collective-permute-start | bytes 18440 | tf_op jit(solution)/shard_map/ppermute | solution.py:13
  78.5 5.1 %collective-permute-start.7 = (f32[6,8,32]{2,1,0:T(8,128)S(1)}, f32[6,8,32]{2,1,0:T(8,128)S(1)}, u32[]{:S(2)}, u32[]{:S(2)}) collective-permute-start(f32[6,8,32]{2,1,0:T(8,128)S(1)} %get-tuple-element.32), channel_id=1, source_target_pairs={{0,64},{32,96},{64,0},{96,32},{128,192},{160,224},{192,128},{224,1... | collective-permute-start | bytes 18440 | tf_op jit(solution)/shard_map/ppermute | solution.py:13
  87.2 10.6 %collective-permute-start.8 = (f32[6,8,32]{2,1,0:T(8,128)}, f32[6,8,32]{2,1,0:T(8,128)}, u32[]{:S(2)}, u32[]{:S(2)}) collective-permute-start(f32[6,8,32]{2,1,0:T(8,128)} %constant_dynamic-update-slice_fusion.12), channel_id=1, source_target_pairs={{0,128},{32,160},{64,192},{96,224},{128,0},{160,32},{192,64},{224,... | collective-permute-start | bytes 18440 | tf_op jit(solution)/shard_map/ppermute | solution.py:13
  90.3 21.6 %copy-start.27 = (s32[1024]{0:T(1024)}, s32[1024]{0:T(1024)S(1)}, u32[]{:S(2)}) copy-start(s32[1024]{0:T(1024)S(1)} %pad_clamp_fusion) | copy-start | bytes 12292
  105.0 6.9 %copy-start.16 = (f32[1,8,32,128]{3,2,1,0:T(8,128)S(1)}, f32[1,8,32,128]{3,2,1,0:T(8,128)}, u32[]{:S(2)}) copy-start(f32[1,8,32,128]{3,2,1,0:T(8,128)} %get-tuple-element.81) | copy-start | bytes 393220
  105.0 6.9 %copy-start.17 = (f32[1,8,32,128]{3,2,1,0:T(8,128)S(1)}, f32[1,8,32,128]{3,2,1,0:T(8,128)}, u32[]{:S(2)}) copy-start(f32[1,8,32,128]{3,2,1,0:T(8,128)} %get-tuple-element.85) | copy-start | bytes 393220
  105.0 6.9 %copy-start.25 = (f32[1,8,32,128]{3,2,1,0:T(8,128)S(1)}, f32[1,8,32,128]{3,2,1,0:T(8,128)}, u32[]{:S(2)}) copy-start(f32[1,8,32,128]{3,2,1,0:T(8,128)} %get-tuple-element.86) | copy-start | bytes 393220
  105.8 16.9 %collective-permute-start.10 = (f32[8,32,1]{2,1,0:T(8,128)}, f32[8,32,1]{2,1,0:T(8,128)}, u32[]{:S(2)}, u32[]{:S(2)}) collective-permute-start(f32[8,32,1]{2,1,0:T(8,128)} %get-tuple-element.120), channel_id=1, source_target_pairs={{32,0},{64,32},{96,64},{128,96},{160,128},{192,160},{224,192},{33,... | collective-permute-start | bytes 3080 | tf_op jit(solution)/shard_map/ppermute | solution.py:26
  109.4 13.2 %collective-permute-start.9 = (f32[8,32,1]{2,1,0:T(8,128)}, f32[8,32,1]{2,1,0:T(8,128)}, u32[]{:S(2)}, u32[]{:S(2)}) collective-permute-start(f32[8,32,1]{2,1,0:T(8,128)} %get-tuple-element.119), channel_id=1, source_target_pairs={{0,32},{32,64},{64,96},{96,128},{128,160},{160,192},{192,224},{1,3... | collective-permute-start | bytes 3080 | tf_op jit(solution)/shard_map/ppermute | solution.py:24
  113.7 37.6 %copy-start.28 = (f32[256]{0:T(256)}, f32[256]{0:T(256)S(1)}, u32[]{:S(2)}) copy-start(f32[256]{0:T(256)S(1)} %gather_fusion) | copy-start | bytes 3076
  113.7 17.6 %copy-start.31 = (f32[16]{0:T(128)S(1)}, f32[16]{0:T(128)}, u32[]{:S(2)}) copy-start(f32[16]{0:T(128)} %copy-done.30) | copy-start | bytes 196
  114.4 16.7 %all-to-all-start.3 = ((f32[32,1,8]{2,1,0:T(1,128)}), f32[32,1,8]{2,1,0:T(1,128)S(1)}, u32[]{:S(2)}, u32[]{:S(2)}) async-start(f32[32,1,8]{2,1,0:T(1,128)} %bitcast.45), calls=%async_computation.3 | async-start | bytes 32768 | tf_op jit(solution)/shard_map/all_to_all | solution.py:198
  124.2 27.1 %collective-permute-start.11 = (f32[8,1,130]{2,1,0:T(1,128)}, f32[8,1,130]{2,1,0:T(1,128)S(1)}, u32[]{:S(2)}, u32[]{:S(2)}) collective-permute-start(f32[8,1,130]{2,1,0:T(1,128)} %get-tuple-element.79), channel_id=1, source_target_pairs={{0,4},{4,8},{8,12},{12,16},{16,20},{20,24},{24,28},{1,5},{5,9},{9,... | collective-permute-start | bytes 12488 | tf_op jit(solution)/shard_map/ppermute | solution.py:24
  127.3 24.0 %collective-permute-start.12 = (f32[8,1,130]{2,1,0:T(1,128)}, f32[8,1,130]{2,1,0:T(1,128)}, u32[]{:S(2)}, u32[]{:S(2)}) collective-permute-start(f32[8,1,130]{2,1,0:T(1,128)} %get-tuple-element.80), channel_id=1, source_target_pairs={{4,0},{8,4},{12,8},{16,12},{20,16},{24,20},{28,24},{5,1},{9,5},{13... | collective-permute-start | bytes 12488 | tf_op jit(solution)/shard_map/ppermute | solution.py:26
  151.3 5.6 %copy-start.37 = (f32[256]{0:T(256)S(1)}, f32[256]{0:T(256)}, u32[]{:S(2)}) copy-start(f32[256]{0:T(256)} %all_to_all.56) | copy-start | bytes 3076
  151.3 5.6 %copy-start.29 = (f32[256]{0:T(256)S(1)}, f32[256]{0:T(256)}, u32[]{:S(2)}) copy-start(f32[256]{0:T(256)} %copy-done.28) | copy-start | bytes 3076
  152.8 7.4 %collective-permute-start.13 = (f32[1,34,130]{2,1,0:T(8,128)}, f32[1,34,130]{2,1,0:T(8,128)}, u32[]{:S(2)}, u32[]{:S(2)}) collective-permute-start(f32[1,34,130]{2,1,0:T(8,128)} %get-tuple-element.77), channel_id=1, source_target_pairs={{0,1},{1,2},{2,3},{4,5},{5,6},{6,7},{8,9},{9,10},{10,11},{12,13},{... | collective-permute-start | bytes 53048 | tf_op jit(solution)/shard_map/ppermute | solution.py:24
  155.6 4.8 %collective-permute-start.14 = (f32[1,34,130]{2,1,0:T(8,128)S(1)}, f32[1,34,130]{2,1,0:T(8,128)}, u32[]{:S(2)}, u32[]{:S(2)}) collective-permute-start(f32[1,34,130]{2,1,0:T(8,128)S(1)} %get-tuple-element.78), channel_id=1, source_target_pairs={{1,0},{2,1},{3,2},{5,4},{6,5},{7,6},{9,8},{10,9},{11,10},{13,12},{... | collective-permute-start | bytes 53048 | tf_op jit(solution)/shard_map/ppermute | solution.py:26
  164.6 9.7 %copy-start.38 = (f32[16]{0:T(128)S(1)}, f32[16]{0:T(128)}, u32[]{:S(2)}) copy-start(f32[16]{0:T(128)} %get-tuple-element.189) | copy-start | bytes 196
  164.9 5.8 %collective-permute-start.15 = (f32[6,8,32]{2,1,0:T(8,128)S(1)}, f32[6,8,32]{2,1,0:T(8,128)S(1)}, u32[]{:S(2)}, u32[]{:S(2)}) collective-permute-start(f32[6,8,32]{2,1,0:T(8,128)S(1)} %constant_dynamic-update-slice_fusion.18), channel_id=1, source_target_pairs={{0,32},{32,0},{64,96},{96,64},{128,160},{160,128},{192,224},{224,1... | collective-permute-start | bytes 18440 | tf_op jit(solution)/shard_map/ppermute | solution.py:13
  170.8 2.8 %collective-permute-start.16 = (f32[6,8,32]{2,1,0:T(8,128)S(1)}, f32[6,8,32]{2,1,0:T(8,128)S(1)}, u32[]{:S(2)}, u32[]{:S(2)}) collective-permute-start(f32[6,8,32]{2,1,0:T(8,128)S(1)} %get-tuple-element.15), channel_id=1, source_target_pairs={{0,64},{32,96},{64,0},{96,32},{128,192},{160,224},{192,128},{224,1... | collective-permute-start | bytes 18440 | tf_op jit(solution)/shard_map/ppermute | solution.py:13
  173.7 4.3 %collective-permute-start.17 = (f32[6,8,32]{2,1,0:T(8,128)S(1)}, f32[6,8,32]{2,1,0:T(8,128)S(1)}, u32[]{:S(2)}, u32[]{:S(2)}) collective-permute-start(f32[6,8,32]{2,1,0:T(8,128)S(1)} %constant_dynamic-update-slice_fusion.30), channel_id=1, source_target_pairs={{0,128},{32,160},{64,192},{96,224},{128,0},{160,32},{192,64},{224,... | collective-permute-start | bytes 18440 | tf_op jit(solution)/shard_map/ppermute | solution.py:13
  182.7 12.9 %copy-start.40 = (f32[4]{0:T(128)S(1)}, f32[4]{0:T(128)}, u32[]{:S(2)}) copy-start(f32[4]{0:T(128)} %copy-done.39) | copy-start | bytes 52
  182.7 12.9 %copy-start.44 = (f32[1,1,4]{2,1,0:T(1,128)S(1)}, f32[1,1,4]{2,1,0:T(1,128)}, u32[]{:S(2)}) copy-start(f32[1,1,4]{2,1,0:T(1,128)} %param.19) | copy-start | bytes 52
  182.7 12.6 %all-to-all-start.5 = ((f32[32,1,8]{2,1,0:T(1,128)}), f32[32,1,8]{2,1,0:T(1,128)S(1)}, u32[]{:S(2)}, u32[]{:S(2)}) async-start(f32[32,1,8]{2,1,0:T(1,128)} %bitcast.85), calls=%async_computation.5 | async-start | bytes 32768 | tf_op jit(solution)/shard_map/all_to_all | solution.py:198
  (20 other events, 36.4 us)
where the time goes:
time: 199 us; the launch traced here: 196 us
  starting transfers between devices  75.7 us (38%)
  waiting for transfers between devices  40.8 us (21%)
  local copies, waits for them, and re-layouts  31.7 us (16%)
  other arithmetic  28.7 us (14%)
  blocking collectives  17.2 us (9%)
  between operations  2.24 us (1%)
    ppermute x6, starting transfers between devices, with_halo(): lax.ppermute(tail, axis, [(i, (i + 1) % count) for i in range(ends)])  18.3 us
    all_to_all x1, blocking collectives, return_pressure(): lax.all_to_all(per_slot, ('gy', 'gz'), split_axis=0, concat_axis=0, tiled...  17.2 us
    ppermute x6, starting transfers between devices, from_partner(): lax.ppermute(x, axis, [(i, i ^ 1 << bit) for i in range(lax.axis_size(axi...  15.7 us
    all_to_all x2, starting transfers between devices, send_pressure(): lax.all_to_all(perforated, ('gy', 'gz'), split_axis=0, concat_axis=0, til...  12.3 us
    all_to_all x1, starting transfers between devices, shards(): lax.all_to_all(local_weight, ('gy', 'gz'), split_axis=0, concat_axis=0, t...  11 us
    ppermute x6, starting transfers between devices, with_halo(): lax.ppermute(head, axis, [((i + 1) % count, i) for i in range(ends)])  10.8 us
    all_to_all x2, waiting for transfers between devices, send_pressure(): lax.all_to_all(perforated, ('gy', 'gz'), split_axis=0, concat_axis=0, til...  10.2 us
    ppermute x6, waiting for transfers between devices, from_partner(): lax.ppermute(x, axis, [(i, i ^ 1 << bit) for i in range(lax.axis_size(axi...  7.63 us
  transfers between devices with their start and end apart: 23, of which 13 were waited for; matrix products, arithmetic and copies ran while one was open for 13% of the time, Pallas kernels for 0%

commit v1 on v0

v1 whole, which is shorter than its diff:
```python
import functools

import jax
import jax.numpy as jnp
from jax import lax
from jax.experimental import pallas as pl
from jax.experimental.pallas import tpu as pltpu
from jax.sharding import PartitionSpec as P

F32 = jnp.float32
BF16 = jnp.bfloat16
MESH = pl.DeviceIdType.MESH
LANES = 128
SEG = 4
BORE = 20.0


def harmonic(a, b):
    return 2.0 * a * b / (a + b)


def lane_of(shape):
    return lax.broadcasted_iota(jnp.int32, shape, len(shape) - 1)


def row_of(shape):
    return lax.broadcasted_iota(jnp.int32, shape, len(shape) - 2)


def split_lanes(x):
    high = x.astype(BF16)
    low = (x - high.astype(F32)).astype(BF16)
    return jnp.concatenate([high, low], axis=1)


def onehot_product(selector, x):
    both = jnp.dot(selector, split_lanes(x), preferred_element_type=F32)
    return both[:, :LANES] + both[:, LANES:]


def lane_spread(x, lane, shape):
    return jnp.broadcast_to(x[:, lane : lane + 1], shape)


def pack_ends(pieces):
    pair = lane_of((8, LANES)) // 2
    packed = jnp.zeros((8, LANES), F32)
    for j, piece in enumerate(pieces):
        packed = jnp.where(pair == j, pltpu.roll(piece, 2 * j + 1, 1), packed)
    return packed


def kernel(
    dims, cell_ref, well_ref, wgt_ref, cnt_ref, bhp_ref, rhs_in, px_in, py_in, pz_in, st_in, p_out, res_out,
    rhs, px, py, pz, st, sig, left, right, ylo, yup, zface, alpha, gamma, inv, low_w, high_w, src, field,
    hot_x, hot_dw, line_sel, line_sel_t,
    yperm, zperm, yp, ysend_perm, ysend_p, zp,
    sw_send, sw_all, row_send, rows_a, rows_b, stat_all, ports_a, ports_b, port_send,
    coef_seg, coef_mine,
    in_sem, out_sem, halo_send, halo_recv, fan_send, fan_recv,
):
    nx, ny, nz, zc, yc, wells = dims
    ng = ny * nz
    lines = zc * yc
    pieces = lines // 8
    mx, my, mz = lax.axis_index("gx"), lax.axis_index("gy"), lax.axis_index("gz")
    mg = my * nz + mz

    loads = [
        pltpu.make_async_copy(a, b, in_sem.at[i])
        for i, (a, b) in enumerate(((py_in, py), (pz_in, pz), (px_in, px), (st_in, st), (rhs_in, rhs)))
    ]
    for load in loads:
        load.start()

    barrier = pltpu.get_barrier_semaphore()

    def greet_x(t, c):
        pl.semaphore_signal(barrier, inc=1, device_id={"gx": lax.rem(mx + t, nx)}, device_id_type=MESH)
        return c

    def greet_group(t, c):
        peer = lax.rem(mg + t, ng)
        pl.semaphore_signal(
            barrier, inc=1, device_id={"gy": lax.div(peer, nz), "gz": lax.rem(peer, nz)}, device_id_type=MESH
        )
        return c

    lax.fori_loop(1, ng, greet_group, 0)
    lax.fori_loop(1, nx, greet_x, 0)

    code = cell_ref[...]
    wellv = well_ref[...]
    wgtv = wgt_ref[...]
    lane8 = lane_of((8, LANES))
    sw_row = jnp.zeros((8, LANES), F32)
    for d in range(ng):
        rows = slice(d * 8, d * 8 + 8)
        c = lane_spread(code, d, (8, LANES))
        w = lane_spread(wgtv, d, (8, LANES))
        x = jnp.bitwise_and(c, LANES - 1)
        hot_x[rows, :] = jnp.where(lane8 == x, 1.0, 0.0)
        mine = jnp.where(lane8 == lane_spread(wellv, d, (8, LANES)) + d * wells, 1.0, 0.0)
        mine = mine * w
        hot_dw[rows, :] = mine
        sw_row = sw_row + mine
    sw_send[0] = jnp.sum(sw_row, axis=0, keepdims=True)
    lane1 = lane_of((1, LANES))
    counts = jnp.zeros((1, LANES), F32)
    bores = jnp.zeros((1, LANES), F32)
    for w in range(wells):
        here = lane1 == mg * wells + w
        counts = jnp.where(here, cnt_ref[0, w].astype(F32), counts)
        bores = jnp.where(here, bhp_ref[0, w], bores)
    sw_send[1] = counts
    sw_send[2] = bores

    def fan_group(source, target, which):
        def step(t, c):
            peer = lax.rem(mg + t, ng)
            pltpu.make_async_remote_copy(
                src_ref=source, dst_ref=target.at[mg], send_sem=fan_send.at[which], recv_sem=fan_recv.at[which],
                device_id={"gy": lax.div(peer, nz), "gz": lax.rem(peer, nz)}, device_id_type=MESH,
            ).start()
            return c

        lax.fori_loop(1, ng, step, 0)

    def fan_x(source, target, which):
        def step(t, c):
            pltpu.make_async_remote_copy(
                src_ref=source, dst_ref=target.at[mx], send_sem=fan_send.at[which], recv_sem=fan_recv.at[which],
                device_id={"gx": lax.rem(mx + t, nx)}, device_id_type=MESH,
            ).start()
            return c

        lax.fori_loop(1, nx, step, 0)

    def fan_wait(target, count, sems, which):
        view = target.at[pl.ds(0, count)]
        pltpu.make_async_copy(view, view, sems.at[which]).wait()

    y_next, y_prev = lax.rem(my + 1, ny), lax.rem(my + ny - 1, ny)
    z_next, z_prev = lax.rem(mz + 1, nz), lax.rem(mz + nz - 1, nz)

    def halo_copy(source, target, which, peer):
        return pltpu.make_async_remote_copy(
            src_ref=source, dst_ref=target, send_sem=halo_send.at[which], recv_sem=halo_recv.at[which],
            device_id=peer, device_id_type=MESH,
        )

    def halos(y_src, y_dst, z_src, z_dst, base):
        last = pl.ds((zc - 1) * yc, yc)
        return [
            halo_copy(y_src.at[0], y_dst.at[1], base, {"gy": y_prev}),
            halo_copy(y_src.at[1], y_dst.at[0], base + 1, {"gy": y_next}),
            halo_copy(z_src.at[pl.ds(0, yc)], z_dst.at[1], base + 2, {"gz": z_prev}),
            halo_copy(z_src.at[last], z_dst.at[0], base + 3, {"gz": z_next}),
        ]

    loads[0].wait()
    loads[1].wait()
    for z in range(zc):
        ysend_perm[0, z] = py[z * yc : z * yc + 1, :]
        ysend_perm[1, z] = py[z * yc + yc - 1 : z * yc + yc, :]

    pl.semaphore_wait(barrier, ng - 1 + nx - 1)
    fan_group(sw_send, sw_all, 0)
    perm_halos = halos(ysend_perm, yperm, pz, zperm, 0)
    for copy in perm_halos:
        copy.start()
    sw_all[mg] = sw_send[...]

    for half in range(lines // LANES):
        for d in range(ng):
            line = jnp.right_shift(lane_spread(code, d, (8, LANES)), 7) - half * LANES
            line_sel[d * 8 : d * 8 + 8, half * LANES : half * LANES + LANES] = jnp.where(lane8 == line, 1.0, 0.0)
    line_sel_t[...] = line_sel[...].T.astype(BF16)

    loads[2].wait()
    loads[3].wait()
    lane_s = lane_of((yc, LANES))
    row_s = row_of((yc, LANES))
    for z in range(zc):
        rows = slice(z * yc, z * yc + yc)
        v = px[rows, :]
        f = jnp.where(lane_s == 0, 0.0, harmonic(pltpu.roll(v, 1, 1), v))
        left[rows, :] = f
        right[rows, :] = pltpu.roll(f, LANES - 1, 1)
    for copy in perm_halos:
        copy.wait_recv()
    for z in range(zc):
        rows = slice(z * yc, z * yc + yc)
        v = py[rows, :]
        below = jnp.where(row_s == 0, yperm[0, z], pltpu.roll(v, 1, 0))
        f = harmonic(below, v)
        f = jnp.where(jnp.logical_and(row_s == 0, my == 0), 0.0, f)
        top = harmonic(py[z * yc + yc - 1 : z * yc + yc, :], yperm[1, z])
        top = jnp.where(my == ny - 1, 0.0, top)
        g = jnp.where(row_s == yc - 1, top, pltpu.roll(f, yc - 1, 0))
        ylo[rows, :] = f
        yup[rows, :] = g
        sig[rows, :] = st[rows, :] + f + g
    before = zperm[0]
    for z in range(zc + 1):
        v = pz[z * yc : z * yc + yc, :] if z < zc else zperm[1]
        f = harmonic(before, v)
        if z == 0:
            f = jnp.where(mz == 0, 0.0, f)
        if z == zc:
            f = jnp.where(mz == nz - 1, 0.0, f)
        zface[z * yc : z * yc + yc, :] = f
        before = v
    for z in range(zc):
        rows = slice(z * yc, z * yc + yc)
        sig[rows, :] = sig[rows, :] + zface[rows, :] + zface[z * yc + yc : z * yc + 2 * yc, :]

    chunk = 64
    lane_c = lane_of((chunk, LANES))
    strides = [1 << i for i in range(7)]

    def reduce_matrix(i, carry):
        rows = pl.ds(pl.multiple_of(i * chunk, chunk), chunk)
        lo, hi, s = left[rows, :], right[rows, :], sig[rows, :]
        for level, stride in enumerate(strides):
            r = 1.0 / (s + lo + hi)
            from_low = lane_c > stride
            from_high = lane_c < LANES - 1 - stride
            a = jnp.where(from_low, lo * pltpu.roll(r, stride, 1), 0.0)
            g = jnp.where(from_high, hi * pltpu.roll(r, LANES - stride, 1), 0.0)
            s = s + a * pltpu.roll(s, stride, 1) + g * pltpu.roll(s, LANES - stride, 1)
            lo = jnp.where(from_low, a * pltpu.roll(lo, stride, 1), lo)
            hi = jnp.where(from_high, g * pltpu.roll(hi, LANES - stride, 1), hi)
            alpha[level, rows, :] = a
            gamma[level, rows, :] = g
        r = 1.0 / (s + lo + hi)
        first, last = lane_c == 0, lane_c == LANES - 1
        end = jnp.logical_or(first, last)
        inv[rows, :] = jnp.where(end, 0.0, r)
        low_w[rows, :] = jnp.where(first, 1.0, jnp.where(last, 0.0, lo * r))
        high_w[rows, :] = jnp.where(last, 1.0, jnp.where(first, 0.0, hi * r))
        sig[rows, :] = s
        right[rows, :] = hi
        return carry

    lax.fori_loop(0, lines // chunk, reduce_matrix, 0)

    def ends_of(ref):
        return pack_ends([ref[j * 8 : j * 8 + 8, :] for j in range(pieces)])

    stat_all[mx, 0] = ends_of(sig) + pltpu.roll(ends_of(px), LANES // 2, 1)
    stat_all[mx, 1] = ends_of(right)
    fan_x(stat_all.at[mx], stat_all, 1)

    fan_wait(sw_all, ng - 1, fan_recv, 0)
    total = jnp.zeros((3, 1, LANES), F32)
    for s in range(ng):
        total = total + sw_all[s]
    count, bore = total[1], total[2]

    def slot_of(g):
        return jnp.floor(g * count * (1.0 / nz))

    layer_slots = [slot_of(float(g)) for g in range(nz)]
    layer_sw = [sum(sw_all[y * nz + g, 0] for y in range(ny)) for g in range(nz)]
    layer_inv = []
    layer_seg = []
    for g in range(nz):
        same = sum(jnp.where(layer_slots[h] == layer_slots[g], layer_sw[h], 0.0) for h in range(nz))
        layer_seg.append(same)
        layer_inv.append(1.0 / (same + BORE))
    my_slot = slot_of(mz.astype(F32))
    my_inv = jnp.zeros((1, LANES), F32)
    for g in range(nz):
        my_inv = jnp.where(mz == g, layer_inv[g], my_inv)
    for g in range(nz):
        coef_seg[g] = layer_inv[g]
        coef_mine[g] = jnp.where(layer_slots[g] == my_slot, 1.0, 0.0) * my_inv
    my_base = BORE * bore * my_inv

    def well_sources(pressure_cols, seg_row):
        drop = seg_row if pressure_cols is None else seg_row - pressure_cols
        back = jnp.sum(hot_dw[...] * drop, axis=1, keepdims=True)
        return onehot_product(line_sel_t[...], hot_x[...] * back)

    def solve_local(b_ref):
        half = lines // 2
        ends = []
        for h in range(2):
            rows = slice(h * half, h * half + half)
            b = b_ref[rows, :]
            for level, stride in enumerate(strides):
                b = b + alpha[level, rows, :] * pltpu.roll(b, stride, 1) + gamma[level, rows, :] * pltpu.roll(
                    b, LANES - stride, 1
                )
            b_ref[rows, :] = b
            ends += [b[j * 8 : j * 8 + 8, :] for j in range(half // 8)]
        packed = pack_ends(ends)
        return packed + pltpu.roll(packed, LANES // 2, 1)

    loads[4].wait()
    src[...] = rhs[...] + well_sources(None, my_base)
    ports_a[mx] = solve_local(src)
    fan_x(ports_a.at[mx], ports_a, 2)

    fan_wait(stat_all, nx - 1, fan_recv, 1)

    def ends_at(k):
        s, c = stat_all[k, 0], stat_all[k, 1]
        return dict(
            sz=s, sf=pltpu.roll(s, LANES - 1, 1), pz=pltpu.roll(s, LANES // 2, 1),
            pf=pltpu.roll(s, LANES // 2 - 1, 1), c=pltpu.roll(c, LANES - 1, 1),
        )

    own = ends_at(mx)

    def walk(direction):
        chain = []
        for t in range(1, nx):
            k = mx + direction * t
            valid = jnp.logical_and(k >= 0, k < nx)
            chain.append((jnp.clip(k, 0, nx - 1), valid))
        blocks = [ends_at(k) for k, _ in chain]
        ground = jnp.zeros((8, LANES), F32)
        factors = [None] * (nx - 1)
        for t in range(nx - 1, 0, -1):
            b = blocks[t - 1]
            nearer = own if t == 1 else blocks[t - 2]
            far, near, edge = ("sf", "sz", ("pz", "pf")) if direction < 0 else ("sz", "sf", ("pf", "pz"))
            face = jnp.where(chain[t - 1][1], harmonic(b[edge[0]], nearer[edge[1]]), 0.0)
            through = b["c"] / (b["c"] + b[far] + ground)
            inner = b[near] + (b[far] + ground) * through
            outward = face / (face + inner)
            ground = inner * outward
            factors[t - 1] = (through, outward)
        reach = jnp.ones((8, LANES), F32)
        weights = []
        for through, outward in factors:
            near_w = reach * outward
            reach = near_w * through
            weights.append((near_w, reach))
        return ground, weights, [k for k, _ in chain]

    ground_l, weights_l, index_l = walk(-1)
    ground_r, weights_r, index_r = walk(1)
    a, e, c = own["sf"] + ground_l, own["sz"] + ground_r, own["c"]
    scale = 1.0 / (a * e + (a + e) * c)
    ff, fz, zz = (e + c) * scale, c * scale, (a + c) * scale
    even = lane8 % 2 == 0
    lower_half = lane8 < LANES // 2

    def weave(z_first, f_first, z_last, f_last):
        first = jnp.where(even, z_first, pltpu.roll(f_first, 1, 1))
        last = jnp.where(even, pltpu.roll(z_last, LANES // 2, 1), pltpu.roll(f_last, LANES // 2 + 1, 1))
        return jnp.where(lower_half, first, last)

    terms = [(mx, weave(fz, ff, zz, fz))]
    for (near_w, far_w), k in zip(weights_l, index_l):
        terms.append((k, weave(ff * near_w, ff * far_w, fz * near_w, fz * far_w)))
    for (near_w, far_w), k in zip(weights_r, index_r):
        terms.append((k, weave(fz * far_w, fz * near_w, zz * far_w, zz * near_w)))

    def join(ports, b_ref, write):
        ends = sum(w * ports[k] for k, w in terms)
        ends = ends + pltpu.roll(ends, LANES - 1, 1)
        for j in range(pieces):
            rows = slice(j * 8, j * 8 + 8)
            first = lane_spread(ends, 2 * j, (8, LANES))
            last = lane_spread(ends, LANES // 2 + 2 * j, (8, LANES))
            write(rows, b_ref[rows, :] * inv[rows, :] + low_w[rows, :] * first + high_w[rows, :] * last)

    def perforated():
        rows = onehot_product(line_sel[...].astype(BF16), field[...])
        cols = jnp.sum(rows * hot_x[...], axis=1, keepdims=True)
        return cols, jnp.sum(hot_dw[...] * cols, axis=0, keepdims=True)

    fan_wait(ports_a, nx - 1, fan_recv, 2)

    def write_first(rows, value):
        field[rows, :] = value

    join(ports_a, src, write_first)
    for z in range(zc):
        ysend_p[0, z] = field[z * yc : z * yc + 1, :]
        ysend_p[1, z] = field[z * yc + yc - 1 : z * yc + yc, :]
    p_halos = halos(ysend_p, yp, field, zp, 4)
    for copy in p_halos:
        copy.start()
    cols, row = perforated()
    row_send[0] = row
    fan_group(row_send.at[0], rows_a, 3)
    rows_a[mg] = row

    for copy in p_halos:
        copy.wait_recv()
    for z in range(zc):
        rows = slice(z * yc, z * yc + yc)
        v = field[rows, :]
        below = jnp.where(row_s == 0, yp[0, z], pltpu.roll(v, 1, 0))
        above = jnp.where(row_s == yc - 1, yp[1, z], pltpu.roll(v, yc - 1, 0))
        under = field[z * yc - yc : z * yc, :] if z > 0 else zp[0]
        over = field[z * yc + yc : z * yc + 2 * yc, :] if z < zc - 1 else zp[1]
        beside = ylo[rows, :] * below + yup[rows, :] * above
        beside = beside + zface[rows, :] * under + zface[z * yc + yc : z * yc + 2 * yc, :] * over
        src[rows, :] = rhs[rows, :] + beside

    fan_wait(rows_a, ng - 1, fan_recv, 3)
    seg_row = my_base
    for g in range(nz):
        seg_row = seg_row + coef_mine[g] * sum(rows_a[y * nz + g] for y in range(ny))
    src[...] = src[...] + well_sources(cols, seg_row)

    ports_b[mx] = solve_local(src)
    fan_x(ports_b.at[mx], ports_b, 4)
    for copy in p_halos:
        copy.wait_send()
    fan_wait(ports_b, nx - 1, fan_recv, 4)

    join(ports_b, src, write_first)
    store = pltpu.make_async_copy(field, p_out, out_sem)
    store.start()
    _, row = perforated()
    row_send[1] = row
    fan_group(row_send.at[1], rows_b, 5)
    rows_b[mg] = row
    fan_wait(rows_b, ng - 1, fan_recv, 5)
    res = jnp.zeros((1, LANES), F32)
    for g in range(nz):
        inflow = sum(rows_b[y * nz + g] - bore * sw_all[y * nz + g, 0] for y in range(ny))
        res = res + coef_seg[g] * inflow
    res_out[...] = res

    store.wait()
    for copy in perm_halos:
        copy.wait_send()
    fan_wait(sw_all, ng - 1, fan_send, 0)
    fan_wait(stat_all, nx - 1, fan_send, 1)
    fan_wait(ports_a, nx - 1, fan_send, 2)
    fan_wait(rows_a, ng - 1, fan_send, 3)
    fan_wait(ports_b, nx - 1, fan_send, 4)
    fan_wait(rows_b, ng - 1, fan_send, 5)


def shards(dims, rhs, perm_x, perm_y, perm_z, storage, perf_cell, perf_well, perf_index, seg_count, bhp):
    nx, ny, nz, zc, yc, wells = dims
    ng = ny * nz
    lines = zc * yc
    perfs = ng * 8
    plane = (lines, LANES)
    flat = [a.reshape(plane) for a in (rhs, perm_x, perm_y, perm_z, storage)]
    slots = [a[0, 0].T for a in (perf_cell, perf_well, perf_index)]
    vmem = pl.BlockSpec(memory_space=pltpu.VMEM)
    smem = pl.BlockSpec(memory_space=pltpu.SMEM)
    anywhere = pl.BlockSpec(memory_space=pl.ANY)
    whole = pltpu.VMEM(plane, F32)
    perf_plane = pltpu.VMEM((perfs, LANES), F32)
    pressure, residual = pl.pallas_call(
        functools.partial(kernel, dims),
        out_shape=(jax.ShapeDtypeStruct(plane, F32), jax.ShapeDtypeStruct((1, LANES), F32)),
        in_specs=[vmem] * 3 + [smem] * 2 + [anywhere] * 5,
        out_specs=(anywhere, vmem),
        scratch_shapes=[whole] * 5
        + [whole] * 5
        + [pltpu.VMEM((lines + yc, LANES), F32)]
        + [pltpu.VMEM((7, lines, LANES), F32)] * 2
        + [whole] * 5
        + [perf_plane] * 2
        + [pltpu.VMEM((perfs, lines), F32), pltpu.VMEM((lines, perfs), BF16)]
        + [pltpu.VMEM((2, zc, 1, LANES), F32), pltpu.VMEM((2, yc, LANES), F32)]
        + [pltpu.VMEM((2, zc, 1, LANES), F32)] * 3
        + [pltpu.VMEM((2, yc, LANES), F32)]
        + [pltpu.VMEM((3, 1, LANES), F32), pltpu.VMEM((ng, 3, 1, LANES), F32)]
        + [pltpu.VMEM((2, 1, LANES), F32)]
        + [pltpu.VMEM((ng, 1, LANES), F32)] * 2
        + [pltpu.VMEM((nx, 2, 8, LANES), F32)]
        + [pltpu.VMEM((nx, 8, LANES), F32)] * 2
        + [pltpu.VMEM((8, LANES), F32)]
        + [pltpu.VMEM((nz, 1, LANES), F32)] * 2
        + [
            pltpu.SemaphoreType.DMA((5,)),
            pltpu.SemaphoreType.DMA,
            pltpu.SemaphoreType.DMA((8,)),
            pltpu.SemaphoreType.DMA((8,)),
            pltpu.SemaphoreType.DMA((6,)),
            pltpu.SemaphoreType.DMA((6,)),
        ],
        compiler_params=pltpu.CompilerParams(
            collective_id=0, has_side_effects=True, vmem_limit_bytes=32 * 1024 * 1024
        ),
        name="sweeps",
    )(*slots, seg_count[0], bhp[0], *flat)
    position = lax.axis_index("gy") * nz + lax.axis_index("gz")
    mine = lax.dynamic_slice(residual, (0, position * wells), (1, wells))
    return pressure.reshape(rhs.shape), mine.reshape(1, 1, wells)


def solution(mesh):
    nx, ny, nz = mesh.shape["gx"], mesh.shape["gy"], mesh.shape["gz"]
    cells = P("gz", "gy", "gx")
    perfs = P("gx", ("gy", "gz"), None, None)
    owned = P("gx", ("gy", "gz"), None)

    def program(rhs, perm_x, perm_y, perm_z, storage, perf_cell, perf_well, perf_index, seg_count, bhp):
        dims = (nx, ny, nz, rhs.shape[0] // nz, rhs.shape[1] // ny, seg_count.shape[-1])
        return jax.shard_map(
            functools.partial(shards, dims),
            mesh=mesh,
            in_specs=(cells,) * 5 + (perfs,) * 3 + (owned,) * 2,
            out_specs=(cells, owned),
            check_vma=False,
        )(rhs, perm_x, perm_y, perm_z, storage, perf_cell, perf_well, perf_index, seg_count, bhp)

    return program
```

time: 199 us -> 48.9 us (0.25); the launches traced: 196 us -> 48.7 us
  starting transfers between devices: 75.7 us -> 0 us
  Pallas kernels: 0 us -> 41.5 us
  waiting for transfers between devices: 40.8 us -> 0 us
  other arithmetic: 28.7 us -> 0 us
  local copies, waits for them, and re-layouts: 31.7 us -> 6.45 us
  blocking collectives: 17.2 us -> 0 us
    ppermute x18 -> x0, starting transfers between devices: 44.7 us -> none  [the longest x6 18.3 us: with_halo(): lax.ppermute(tail, axis, [(i, (i + 1) % count) for i in range(ends)])]
    pallas_call x0 -> x1, Pallas kernels: none -> 41.5 us  [shards(): pl.pallas_call(functools.partial(kernel, dims), out_shape=(jax.ShapeDtype...]
    all_to_all x5 -> x0, starting transfers between devices: 31 us -> none  [the longest x2 12.3 us: send_pressure(): lax.all_to_all(perforated, ('gy', 'gz'), split_axis=0, concat_axis=0, til...]
    all_to_all x5 -> x0, waiting for transfers between devices: 28.8 us -> none  [the longest x2 10.2 us: send_pressure(): lax.all_to_all(perforated, ('gy', 'gz'), split_axis=0, concat_axis=0, til...]
    all_to_all x1 -> x0, blocking collectives: 17.2 us -> none  [return_pressure(): lax.all_to_all(per_slot, ('gy', 'gz'), split_axis=0, concat_axis=0, tiled...]
    squeeze x35 -> x0, local copies, waits for them, and re-layouts: 14.2 us -> none  [the longest x8 2.81 us: unpack_group(): stacked[0]]
    ppermute x18 -> x0, waiting for transfers between devices: 12 us -> none  [the longest x6 7.63 us: from_partner(): lax.ppermute(x, axis, [(i, i ^ 1 << bit) for i in range(lax.axis_size(axi...]
    slice x40 -> x0, local copies, waits for them, and re-layouts: 6.33 us -> none  [the longest x19 2.38 us: shifted(): return jnp.concatenate([filled, values[..., :-stride]], axis=-1)]
  transfers between devices with their start and end apart: 23 -> 0, of which waited for: 13 -> 0; matrix products, arithmetic and copies ran while one was open for 13% -> 0% of each run, Pallas kernels for 0% -> 0%
where the time goes in v1:
time: 48.9 us; the launch traced here: 48.7 us
  Pallas kernels  41.5 us (85%)
  local copies, waits for them, and re-layouts  6.45 us (13%)
  between operations  0.7 us (1%)
    pallas_call x1, Pallas kernels, shards(): pl.pallas_call(functools.partial(kernel, dims), out_shape=(jax.ShapeDtype...  41.5 us
    unnamed x21, local copies, waits for them, and re-layouts  5.86 us

profile of v1, /device:TPU:1, one launch (start us, length us, event | category | flops | bytes accessed | tf_op | source)
XLA Modules:
  0.0 48.7 jit_solution(3525497389080001390)
XLA Ops:
  0.6 0.0 copy-start.7
  0.7 0.0 copy-start.6
  0.7 0.0 copy-start.5
  0.7 0.0 copy-start.8
  0.7 0.0 copy-start.9
  0.7 0.6 %copy-done.7 = f32[1,1,32,8]{2,3,1,0:T(8,128)S(1)} copy-done((f32[1,1,32,8]{2,3,1,0:T(8,128)S(1)}, f32[1,1,32,8]{2,3,1,0:T(8,128)}, u32[]{:S(2)}) %copy-start.7) | copy-done | bytes 1048
  1.3 0.0 copy-done.6
  1.3 0.0 copy-done.5
  1.4 0.0 copy-done.8
  1.4 0.0 copy-done.9
  1.4 0.0 copy-start
  1.4 0.9 %copy-done = f32[8,32,128]{2,1,0:T(8,128)S(1)} copy-done((f32[8,32,128]{2,1,0:T(8,128)S(1)}, f32[8,32,128]{2,1,0:T(8,128)}, u32[]{:S(2)}) %copy-start) | copy-done | bytes 131096
  2.3 0.0 copy-start.1
  2.3 0.9 %copy-done.1 = f32[8,32,128]{2,1,0:T(8,128)S(1)} copy-done((f32[8,32,128]{2,1,0:T(8,128)S(1)}, f32[8,32,128]{2,1,0:T(8,128)}, u32[]{:S(2)}) %copy-start.1) | copy-done | bytes 131096
  3.2 0.0 copy-start.2
  3.2 0.9 %copy-done.2 = f32[8,32,128]{2,1,0:T(8,128)S(1)} copy-done((f32[8,32,128]{2,1,0:T(8,128)S(1)}, f32[8,32,128]{2,1,0:T(8,128)}, u32[]{:S(2)}) %copy-start.2) | copy-done | bytes 131096
  4.1 0.0 copy-start.3
  4.1 0.9 %copy-done.3 = f32[8,32,128]{2,1,0:T(8,128)S(1)} copy-done((f32[8,32,128]{2,1,0:T(8,128)S(1)}, f32[8,32,128]{2,1,0:T(8,128)}, u32[]{:S(2)}) %copy-start.3) | copy-done | bytes 131096
  5.0 0.0 copy-start.4
  5.0 0.9 %copy-done.4 = f32[8,32,128]{2,1,0:T(8,128)S(1)} copy-done((f32[8,32,128]{2,1,0:T(8,128)S(1)}, f32[8,32,128]{2,1,0:T(8,128)}, u32[]{:S(2)}) %copy-start.4) | copy-done | bytes 131096
  5.9 41.5 %sweeps.1 = (f32[256,128]{1,0:T(8,128)S(1)}, f32[1,128]{1,0:T(1,128)S(1)}) custom-call(s32[8,32]{1,0:T(8,128)S(1)} %bitcast.25, s32[8,32]{1,0:T(8,128)S(1)} %bitcast.26, f32[8,32]{1,0:T(8,128)S(1)} %bitcast.27, s32[1,4]{1,0:T(1,128)S(1)} %bitcast.28, f32[1,4]{1,0:T(1,128)S(1)} %bitcast.29, f32[256,128]{1,0:T(8,128)S(1)} %bitcast.20, ...), custom_call_target="tpu_custom_call" | custom-call | tf_op jit(solution)/shard_map/sweeps/pallas_call | solution.py:457
  47.4 0.6 %dynamic-slice_bitcast_fusion = f32[1,1,4]{2,1,0:T(1,128)} fusion(f32[1,128]{1,0:T(1,128)S(1)} %get-tuple-element.5, s32[]{:T(128)S(6)} %select_n.3), kind=kLoop, calls=%fused_computation | loop fusion | bytes 36 | tf_op jit(solution)/shard_map/reshape | solution.py:494
  48.0 0.7 %copy.13 = f32[8,32,128]{2,1,0:T(8,128)} copy(f32[8,32,128]{2,1,0:T(8,128)S(1)} %bitcast.19) | data formatting | bytes 262144
Async XLA Ops:
  0.6 0.7 %copy-start.7 = (f32[1,1,32,8]{2,3,1,0:T(8,128)S(1)}, f32[1,1,32,8]{2,3,1,0:T(8,128)}, u32[]{:S(2)}) copy-start(f32[1,1,32,8]{2,3,1,0:T(8,128)} %param.17) | copy-start | bytes 3076
  0.7 0.7 %copy-start.6 = (s32[1,1,32,8]{2,3,1,0:T(8,128)S(1)}, s32[1,1,32,8]{2,3,1,0:T(8,128)}, u32[]{:S(2)}) copy-start(s32[1,1,32,8]{2,3,1,0:T(8,128)} %param.16) | copy-start | bytes 3076
  0.7 0.7 %copy-start.5 = (s32[1,1,32,8]{2,3,1,0:T(8,128)S(1)}, s32[1,1,32,8]{2,3,1,0:T(8,128)}, u32[]{:S(2)}) copy-start(s32[1,1,32,8]{2,3,1,0:T(8,128)} %param.15) | copy-start | bytes 3076
  0.7 0.7 %copy-start.8 = (s32[1,1,4]{2,1,0:T(1,128)S(1)}, s32[1,1,4]{2,1,0:T(1,128)}, u32[]{:S(2)}) copy-start(s32[1,1,4]{2,1,0:T(1,128)} %param.18) | copy-start | bytes 52
  0.7 0.7 %copy-start.9 = (f32[1,1,4]{2,1,0:T(1,128)S(1)}, f32[1,1,4]{2,1,0:T(1,128)}, u32[]{:S(2)}) copy-start(f32[1,1,4]{2,1,0:T(1,128)} %param.19) | copy-start | bytes 52
  1.4 0.9 %copy-start = (f32[8,32,128]{2,1,0:T(8,128)S(1)}, f32[8,32,128]{2,1,0:T(8,128)}, u32[]{:S(2)}) copy-start(f32[8,32,128]{2,1,0:T(8,128)} %param.10) | copy-start | bytes 393220
  2.3 0.9 %copy-start.1 = (f32[8,32,128]{2,1,0:T(8,128)S(1)}, f32[8,32,128]{2,1,0:T(8,128)}, u32[]{:S(2)}) copy-start(f32[8,32,128]{2,1,0:T(8,128)} %param.11) | copy-start | bytes 393220
  3.2 0.9 %copy-start.2 = (f32[8,32,128]{2,1,0:T(8,128)S(1)}, f32[8,32,128]{2,1,0:T(8,128)}, u32[]{:S(2)}) copy-start(f32[8,32,128]{2,1,0:T(8,128)} %param.12) | copy-start | bytes 393220
  4.1 0.9 %copy-start.3 = (f32[8,32,128]{2,1,0:T(8,128)S(1)}, f32[8,32,128]{2,1,0:T(8,128)}, u32[]{:S(2)}) copy-start(f32[8,32,128]{2,1,0:T(8,128)} %param.13) | copy-start | bytes 393220
  5.0 0.9 %copy-start.4 = (f32[8,32,128]{2,1,0:T(8,128)S(1)}, f32[8,32,128]{2,1,0:T(8,128)}, u32[]{:S(2)}) copy-start(f32[8,32,128]{2,1,0:T(8,128)} %param.14) | copy-start | bytes 393220

commit v2 on v1

--- a/solution.py
+++ b/solution.py
@@ -51,13 +51,13 @@
 
 
 def kernel(
-    dims, cell_ref, well_ref, wgt_ref, cnt_ref, bhp_ref, rhs_in, px_in, py_in, pz_in, st_in, p_out, res_out,
-    rhs, px, py, pz, st, sig, left, right, ylo, yup, zface, alpha, gamma, inv, low_w, high_w, src, field,
+    dims, cell_in, well_in, wgt_in, cnt_in, bhp_in, rhs_in, px_in, py_in, pz_in, st_in, p_out, res_out,
+    cell_ref, well_ref, wgt_ref, cnt_ref, bhp_ref, rhs, px, py, pz, st, sig, left, right, ylo, yup, zface, alpha, gamma, inv, low_w, high_w, src, field,
     hot_x, hot_dw, line_sel, line_sel_t,
     yperm, zperm, yp, ysend_perm, ysend_p, zp,
     sw_send, sw_all, row_send, rows_a, rows_b, stat_all, ports_a, ports_b, port_send,
     coef_seg, coef_mine,
-    in_sem, out_sem, halo_send, halo_recv, fan_send, fan_recv,
+    in_sem, halo_send, halo_recv, fan_send, fan_recv,
 ):
     nx, ny, nz, zc, yc, wells = dims
     ng = ny * nz
@@ -68,9 +68,14 @@
 
     loads = [
         pltpu.make_async_copy(a, b, in_sem.at[i])
-        for i, (a, b) in enumerate(((py_in, py), (pz_in, pz), (px_in, px), (st_in, st), (rhs_in, rhs)))
+        for i, (a, b) in enumerate(
+            (
+                (py_in, py), (pz_in, pz), (px_in, px), (st_in, st), (rhs_in, rhs),
+                (cell_in, cell_ref), (well_in, well_ref), (wgt_in, wgt_ref), (cnt_in, cnt_ref), (bhp_in, bhp_ref),
+            )
+        )
     ]
-    for load in loads:
+    for load in loads[5:] + loads[:5]:
         load.start()
 
     barrier = pltpu.get_barrier_semaphore()
@@ -89,6 +94,8 @@
     lax.fori_loop(1, ng, greet_group, 0)
     lax.fori_loop(1, nx, greet_x, 0)
 
+    for load in loads[5:]:
+        load.wait()
     code = cell_ref[...]
     wellv = well_ref[...]
     wgtv = wgt_ref[...]
@@ -115,26 +122,26 @@
     sw_send[1] = counts
     sw_send[2] = bores
 
+    def ring(offset, size):
+        return min(offset, size - offset)
+
+    group_offsets = [(dy, dz) for dy in range(ny) for dz in range(nz) if (dy, dz) != (0, 0)]
+    group_offsets.sort(key=lambda o: -(ring(o[0], ny) + ring(o[1], nz)))
+    x_offsets = sorted(range(1, nx), key=lambda o: -ring(o, nx))
+
+    def fan(peers, source, target, which):
+        for peer in peers:
+            pltpu.make_async_remote_copy(
+                src_ref=source, dst_ref=target, send_sem=fan_send.at[which], recv_sem=fan_recv.at[which],
+                device_id=peer, device_id_type=MESH,
+            ).start()
+
     def fan_group(source, target, which):
-        def step(t, c):
-            peer = lax.rem(mg + t, ng)
-            pltpu.make_async_remote_copy(
-                src_ref=source, dst_ref=target.at[mg], send_sem=fan_send.at[which], recv_sem=fan_recv.at[which],
-                device_id={"gy": lax.div(peer, nz), "gz": lax.rem(peer, nz)}, device_id_type=MESH,
-            ).start()
-            return c
-
-        lax.fori_loop(1, ng, step, 0)
+        peers = [{"gy": lax.rem(my + dy, ny), "gz": lax.rem(mz + dz, nz)} for dy, dz in group_offsets]
+        fan(peers, source, target.at[mg], which)
 
     def fan_x(source, target, which):
-        def step(t, c):
-            pltpu.make_async_remote_copy(
-                src_ref=source, dst_ref=target.at[mx], send_sem=fan_send.at[which], recv_sem=fan_recv.at[which],
-                device_id={"gx": lax.rem(mx + t, nx)}, device_id_type=MESH,
-            ).start()
-            return c
-
-        lax.fori_loop(1, nx, step, 0)
+        fan([{"gx": lax.rem(mx + dx, nx)} for dx in x_offsets], source, target.at[mx], which)
 
     def fan_wait(target, count, sems, which):
         view = target.at[pl.ds(0, count)]
@@ -360,33 +367,30 @@
     for (near_w, far_w), k in zip(weights_r, index_r):
         terms.append((k, weave(fz * far_w, fz * near_w, zz * far_w, zz * near_w)))
 
-    def join(ports, b_ref, write):
+    def join(ports, b_ref, target):
         ends = sum(w * ports[k] for k, w in terms)
         ends = ends + pltpu.roll(ends, LANES - 1, 1)
         for j in range(pieces):
             rows = slice(j * 8, j * 8 + 8)
             first = lane_spread(ends, 2 * j, (8, LANES))
             last = lane_spread(ends, LANES // 2 + 2 * j, (8, LANES))
-            write(rows, b_ref[rows, :] * inv[rows, :] + low_w[rows, :] * first + high_w[rows, :] * last)
-
-    def perforated():
-        rows = onehot_product(line_sel[...].astype(BF16), field[...])
+            target[rows, :] = b_ref[rows, :] * inv[rows, :] + low_w[rows, :] * first + high_w[rows, :] * last
+
+    def perforated(values):
+        rows = onehot_product(line_sel[...].astype(BF16), values[...])
         cols = jnp.sum(rows * hot_x[...], axis=1, keepdims=True)
         return cols, jnp.sum(hot_dw[...] * cols, axis=0, keepdims=True)
 
     fan_wait(ports_a, nx - 1, fan_recv, 2)
 
-    def write_first(rows, value):
-        field[rows, :] = value
-
-    join(ports_a, src, write_first)
+    join(ports_a, src, field)
     for z in range(zc):
         ysend_p[0, z] = field[z * yc : z * yc + 1, :]
         ysend_p[1, z] = field[z * yc + yc - 1 : z * yc + yc, :]
     p_halos = halos(ysend_p, yp, field, zp, 4)
     for copy in p_halos:
         copy.start()
-    cols, row = perforated()
+    cols, row = perforated(field)
     row_send[0] = row
     fan_group(row_send.at[0], rows_a, 3)
     rows_a[mg] = row
@@ -412,14 +416,10 @@
 
     ports_b[mx] = solve_local(src)
     fan_x(ports_b.at[mx], ports_b, 4)
-    for copy in p_halos:
-        copy.wait_send()
     fan_wait(ports_b, nx - 1, fan_recv, 4)
 
-    join(ports_b, src, write_first)
-    store = pltpu.make_async_copy(field, p_out, out_sem)
-    store.start()
-    _, row = perforated()
+    join(ports_b, src, p_out)
+    _, row = perforated(p_out)
     row_send[1] = row
     fan_group(row_send.at[1], rows_b, 5)
     rows_b[mg] = row
@@ -428,10 +428,9 @@
     for g in range(nz):
         inflow = sum(rows_b[y * nz + g] - bore * sw_all[y * nz + g, 0] for y in range(ny))
         res = res + coef_seg[g] * inflow
-    res_out[...] = res
-
-    store.wait()
-    for copy in perm_halos:
+    res_out[...] = pltpu.roll(res, lax.rem(LANES - mg * wells, LANES), 1)[:, :wells]
+
+    for copy in perm_halos + p_halos:
         copy.wait_send()
     fan_wait(sw_all, ng - 1, fan_send, 0)
     fan_wait(stat_all, nx - 1, fan_send, 1)
@@ -449,17 +448,19 @@
     plane = (lines, LANES)
     flat = [a.reshape(plane) for a in (rhs, perm_x, perm_y, perm_z, storage)]
     slots = [a[0, 0].T for a in (perf_cell, perf_well, perf_index)]
+    operands = [pltpu.with_memory_space_constraint(a, pltpu.HBM) for a in (*slots, seg_count[0], bhp[0], *flat)]
     vmem = pl.BlockSpec(memory_space=pltpu.VMEM)
-    smem = pl.BlockSpec(memory_space=pltpu.SMEM)
-    anywhere = pl.BlockSpec(memory_space=pl.ANY)
+    hbm = pl.BlockSpec(memory_space=pltpu.HBM)
     whole = pltpu.VMEM(plane, F32)
     perf_plane = pltpu.VMEM((perfs, LANES), F32)
     pressure, residual = pl.pallas_call(
         functools.partial(kernel, dims),
-        out_shape=(jax.ShapeDtypeStruct(plane, F32), jax.ShapeDtypeStruct((1, LANES), F32)),
-        in_specs=[vmem] * 3 + [smem] * 2 + [anywhere] * 5,
-        out_specs=(anywhere, vmem),
-        scratch_shapes=[whole] * 5
+        out_shape=(pltpu.VMEM(plane, F32), pltpu.VMEM((1, wells), F32)),
+        in_specs=[hbm] * 10,
+        out_specs=(vmem, vmem),
+        scratch_shapes=[pltpu.VMEM((8, ng), jnp.int32)] * 2
+        + [pltpu.VMEM((8, ng), F32), pltpu.SMEM((1, wells), jnp.int32), pltpu.SMEM((1, wells), F32)]
+        + [whole] * 5
         + [whole] * 5
         + [pltpu.VMEM((lines + yc, LANES), F32)]
         + [pltpu.VMEM((7, lines, LANES), F32)] * 2
@@ -477,8 +478,7 @@
         + [pltpu.VMEM((8, LANES), F32)]
         + [pltpu.VMEM((nz, 1, LANES), F32)] * 2
         + [
-            pltpu.SemaphoreType.DMA((5,)),
-            pltpu.SemaphoreType.DMA,
+            pltpu.SemaphoreType.DMA((10,)),
             pltpu.SemaphoreType.DMA((8,)),
             pltpu.SemaphoreType.DMA((8,)),
             pltpu.SemaphoreType.DMA((6,)),
@@ -488,10 +488,8 @@
             collective_id=0, has_side_effects=True, vmem_limit_bytes=32 * 1024 * 1024
         ),
         name="sweeps",
-    )(*slots, seg_count[0], bhp[0], *flat)
-    position = lax.axis_index("gy") * nz + lax.axis_index("gz")
-    mine = lax.dynamic_slice(residual, (0, position * wells), (1, wells))
-    return pressure.reshape(rhs.shape), mine.reshape(1, 1, wells)
+    )(*operands)
+    return pressure.reshape(rhs.shape), residual.reshape(1, 1, wells)
 
 
 def solution(mesh):

time: 48.9 us -> 41.4 us (0.85)
  local copies, waits for them, and re-layouts: 6.45 us -> 1.17 us
  Pallas kernels: 41.5 us -> 39.5 us
    unnamed x21 -> x2, local copies, waits for them, and re-layouts: 5.86 us -> 1.17 us
    pallas_call x1, Pallas kernels: 41.5 us -> 39.5 us  [shards(): pl.pallas_call(functools.partial(kernel, dims), out_shape=(pltpu.VMEM(pla...]
    reshape x1 -> x0, local copies, waits for them, and re-layouts: 0.59 us -> none  [shards(): return (pressure.reshape(rhs.shape), mine.reshape(1, 1, wells))]
where the time goes in v2:
time: 41.4 us; the launch traced here: 41.3 us
  Pallas kernels  39.5 us (95%)
  local copies, waits for them, and re-layouts  1.17 us (3%)
  between operations  0.64 us (2%)
    pallas_call x1, Pallas kernels, shards(): pl.pallas_call(functools.partial(kernel, dims), out_shape=(pltpu.VMEM(pla...  39.5 us
    unnamed x2, local copies, waits for them, and re-layouts  1.17 us

profile of v2, /device:TPU:1, one launch (start us, length us, event | category | flops | bytes accessed | tf_op | source)
XLA Modules:
  0.0 41.3 jit_solution(13625965406176360112)
XLA Ops:
  0.6 39.5 %sweeps.1 = (f32[256,128]{1,0:T(8,128)S(1)}, f32[1,4]{1,0:T(1,128)S(1)}) custom-call(s32[8,32]{1,0:T(8,128)} %bitcast.25, s32[8,32]{1,0:T(8,128)} %bitcast.26, f32[8,32]{1,0:T(8,128)} %bitcast.27, s32[1,4]{1,0:T(1,128)} %bitcast.28, f32[1,4]{1,0:T(1,128)} %bitcast.29, f32[256,128]{1,0:T(8,128)} %bitcast.20, f32[256,128]{1,0:T(8,128)} %bitcast.21, ...), custom_call_target="tpu_custom_call" | custom-call | tf_op jit(solution)/shard_map/sweeps/pallas_call | solution.py:456
  40.1 0.7 %copy.14 = f32[8,32,128]{2,1,0:T(8,128)} copy(f32[8,32,128]{2,1,0:T(8,128)S(1)} %bitcast.18) | data formatting | bytes 262144
  40.8 0.5 %copy.15 = f32[1,1,4]{2,1,0:T(1,128)} copy(f32[1,1,4]{2,1,0:T(1,128)S(1)} %bitcast.19) | data formatting | bytes 32

commit v3 on v2

v3 whole, which is shorter than its diff:
```python
import functools

import jax
import jax.numpy as jnp
from jax import lax
from jax.experimental import pallas as pl
from jax.experimental.pallas import tpu as pltpu
from jax.sharding import PartitionSpec as P

F32 = jnp.float32
BF16 = jnp.bfloat16
MESH = pl.DeviceIdType.MESH
LANES = 128
SEG = 4
BORE = 20.0


def harmonic(a, b):
    return 2.0 * a * b / (a + b)


def lane_of(shape):
    return lax.broadcasted_iota(jnp.int32, shape, len(shape) - 1)


def row_of(shape):
    return lax.broadcasted_iota(jnp.int32, shape, len(shape) - 2)


def split_lanes(x):
    high = x.astype(BF16)
    low = (x - high.astype(F32)).astype(BF16)
    return jnp.concatenate([high, low], axis=1)


def onehot_product(selector, x):
    both = jnp.dot(selector, split_lanes(x), preferred_element_type=F32)
    return both[:, :LANES] + both[:, LANES:]


def lane_spread(x, lane, shape):
    return jnp.broadcast_to(x[:, lane : lane + 1], shape)


def pack_ends(pieces):
    pair = lane_of((8, LANES)) // 2
    packed = jnp.zeros((8, LANES), F32)
    for j, piece in enumerate(pieces):
        packed = jnp.where(pair == j, pltpu.roll(piece, 2 * j + 1, 1), packed)
    return packed


def kernel(
    dims, cell_in, well_in, wgt_in, cnt_in, bhp_in, rhs_in, px_in, py_in, pz_in, st_in, p_out, res_out,
    cell_ref, well_ref, wgt_ref, cnt_ref, bhp_ref, rhs, px, py, pz, st,
    sig, left, right, ylo, yup, zface, low_m, high_m, recip, inv, low_w, high_w, src, field,
    hot_x, hot_dw, line_sel, line_sel_t, reach_first, reach_last,
    yperm, zperm, yp, ysend_perm, ysend_p, zp,
    sw_send, sw_all, row_send, rows_a, rows_b, stat_all, ports_a, ports_b,
    in_sem, halo_send, halo_recv, fan_send, fan_recv,
):
    nx, ny, nz, zc, yc, wells = dims
    ng = ny * nz
    lines = zc * yc
    pieces = lines // 8
    mx, my, mz = lax.axis_index("gx"), lax.axis_index("gy"), lax.axis_index("gz")
    mg = my * nz + mz

    def ring(offset, size):
        return min(offset, size - offset)

    group_offsets = [(dy, dz) for dy in range(ny) for dz in range(nz) if (dy, dz) != (0, 0)]
    group_offsets.sort(key=lambda o: -(ring(o[0], ny) + ring(o[1], nz)))
    group_peers = [{"gy": lax.rem(my + dy, ny), "gz": lax.rem(mz + dz, nz)} for dy, dz in group_offsets]
    x_offsets = sorted(range(1, nx), key=lambda o: -ring(o, nx))
    x_peers = [{"gx": lax.rem(mx + dx, nx)} for dx in x_offsets]

    barrier = pltpu.get_barrier_semaphore()
    for peer in group_peers + x_peers:
        pl.semaphore_signal(barrier, inc=1, device_id=peer, device_id_type=MESH)

    loads = [
        pltpu.make_async_copy(a, b, in_sem.at[i])
        for i, (a, b) in enumerate(
            (
                (py_in, py), (pz_in, pz), (px_in, px), (st_in, st), (rhs_in, rhs),
                (cell_in, cell_ref), (well_in, well_ref), (wgt_in, wgt_ref), (cnt_in, cnt_ref), (bhp_in, bhp_ref),
            )
        )
    ]
    for load in loads[5:] + loads[:5]:
        load.start()

    def fan(peers, source, target, which):
        for peer in peers:
            pltpu.make_async_remote_copy(
                src_ref=source, dst_ref=target, send_sem=fan_send.at[which], recv_sem=fan_recv.at[which],
                device_id=peer, device_id_type=MESH,
            ).start()

    def fan_wait(target, count, sems, which):
        view = target.at[pl.ds(0, count)]
        pltpu.make_async_copy(view, view, sems.at[which]).wait()

    y_next, y_prev = lax.rem(my + 1, ny), lax.rem(my + ny - 1, ny)
    z_next, z_prev = lax.rem(mz + 1, nz), lax.rem(mz + nz - 1, nz)

    def halos(y_src, y_dst, z_src, z_dst, base):
        last = pl.ds((zc - 1) * yc, yc)
        routes = (
            (y_src.at[0], y_dst.at[1], {"gy": y_prev}),
            (y_src.at[1], y_dst.at[0], {"gy": y_next}),
            (z_src.at[pl.ds(0, yc)], z_dst.at[1], {"gz": z_prev}),
            (z_src.at[last], z_dst.at[0], {"gz": z_next}),
        )
        return [
            pltpu.make_async_remote_copy(
                src_ref=a, dst_ref=b, send_sem=halo_send.at[base + i], recv_sem=halo_recv.at[base + i],
                device_id=peer, device_id_type=MESH,
            )
            for i, (a, b, peer) in enumerate(routes)
        ]

    for load in loads[5:]:
        load.wait()
    code = cell_ref[...]
    wellv = well_ref[...]
    wgtv = wgt_ref[...]
    piece = (8, LANES)
    lane8 = lane_of(piece)
    sw_row = jnp.zeros(piece, F32)
    for d in range(ng):
        mine = lane8 == lane_spread(wellv, d, piece) + d * wells
        mine = jnp.where(mine, lane_spread(wgtv, d, piece), 0.0)
        hot_dw[d * 8 : d * 8 + 8, :] = mine
        sw_row = sw_row + mine
    sw_send[0] = jnp.sum(sw_row, axis=0, keepdims=True)
    lane1 = lane_of((1, LANES))
    counts = jnp.zeros((1, LANES), F32)
    bores = jnp.zeros((1, LANES), F32)
    for w in range(wells):
        here = lane1 == mg * wells + w
        counts = jnp.where(here, cnt_ref[0, w].astype(F32), counts)
        bores = jnp.where(here, bhp_ref[0, w], bores)
    sw_send[1] = counts
    sw_send[2] = bores

    loads[0].wait()
    loads[1].wait()
    for z in range(zc):
        ysend_perm[0, z] = py[z * yc : z * yc + 1, :]
        ysend_perm[1, z] = py[z * yc + yc - 1 : z * yc + yc, :]

    pl.semaphore_wait(barrier, ng - 1 + nx - 1)
    perm_halos = halos(ysend_perm, yperm, pz, zperm, 0)
    for copy in perm_halos:
        copy.start()
    fan(group_peers, sw_send, sw_all.at[mg], 0)
    sw_all[mg] = sw_send[...]

    loads[2].wait()
    loads[3].wait()
    lane_s = lane_of((yc, LANES))
    row_s = row_of((yc, LANES))
    for z in range(zc):
        rows = slice(z * yc, z * yc + yc)
        v = px[rows, :]
        f = jnp.where(lane_s == 0, 0.0, harmonic(pltpu.roll(v, 1, 1), v))
        left[rows, :] = f
        right[rows, :] = pltpu.roll(f, LANES - 1, 1)
        v = py[rows, :]
        f = harmonic(pltpu.roll(v, 1, 0), v)
        ylo[rows, :] = f
        if z > 0:
            zface[rows, :] = harmonic(pz[z * yc - yc : z * yc, :], pz[rows, :])
    for copy in perm_halos:
        copy.wait_recv()
    zface[0:yc, :] = jnp.where(mz == 0, 0.0, harmonic(zperm[0], pz[0:yc, :]))
    zface[lines : lines + yc, :] = jnp.where(mz == nz - 1, 0.0, harmonic(pz[lines - yc : lines, :], zperm[1]))
    for z in range(zc):
        rows = slice(z * yc, z * yc + yc)
        low = jnp.where(my == 0, 0.0, harmonic(yperm[0, z], py[z * yc : z * yc + 1, :]))
        top = jnp.where(my == ny - 1, 0.0, harmonic(py[z * yc + yc - 1 : z * yc + yc, :], yperm[1, z]))
        f = jnp.where(row_s == 0, low, ylo[rows, :])
        g = jnp.where(row_s == yc - 1, top, pltpu.roll(f, yc - 1, 0))
        ylo[rows, :] = f
        yup[rows, :] = g
        sig[rows, :] = st[rows, :] + f + g + zface[rows, :] + zface[z * yc + yc : z * yc + 2 * yc, :]

    chunk = 128
    lane_c = lane_of((chunk, LANES))
    strides = [1 << i for i in range(7)]

    def reduce_matrix(i, carry):
        rows = pl.ds(pl.multiple_of(i * chunk, chunk), chunk)
        lo, hi, s = left[rows, :], right[rows, :], sig[rows, :]
        for level, stride in enumerate(strides):
            r = 1.0 / (s + lo + hi)
            from_low = lane_c > stride
            from_high = lane_c < LANES - 1 - stride
            a = jnp.where(from_low, lo, 0.0)
            g = jnp.where(from_high, hi, 0.0)
            low_m[level, rows, :] = a
            high_m[level, rows, :] = g
            recip[level, rows, :] = r
            q = s * r
            s = s + a * pltpu.roll(q, stride, 1) + g * pltpu.roll(q, LANES - stride, 1)
            lo = jnp.where(from_low, lo * pltpu.roll(lo * r, stride, 1), lo)
            hi = jnp.where(from_high, hi * pltpu.roll(hi * r, LANES - stride, 1), hi)
        r = 1.0 / (s + lo + hi)
        first, last = lane_c == 0, lane_c == LANES - 1
        inv[rows, :] = jnp.where(jnp.logical_or(first, last), 0.0, r)
        low_w[rows, :] = jnp.where(first, 1.0, jnp.where(last, 0.0, lo * r))
        high_w[rows, :] = jnp.where(last, 1.0, jnp.where(first, 0.0, hi * r))
        sig[rows, :] = s
        right[rows, :] = hi
        return carry

    lax.fori_loop(0, lines // chunk, reduce_matrix, 0)

    def ends_of(ref):
        return pack_ends([ref[j * 8 : j * 8 + 8, :] for j in range(pieces)])

    stat_all[mx, 0] = ends_of(sig) + pltpu.roll(ends_of(px), LANES // 2, 1)
    stat_all[mx, 1] = ends_of(right)
    fan(x_peers, stat_all.at[mx], stat_all.at[mx], 1)

    for d in range(ng):
        c = lane_spread(code, d, piece)
        rows = slice(d * 8, d * 8 + 8)
        hot_x[rows, :] = jnp.where(lane8 == jnp.bitwise_and(c, LANES - 1), 1.0, 0.0)
        for half in range(lines // LANES):
            hit = lane8 == jnp.right_shift(c, 7) - half * LANES
            line_sel[rows, half * LANES : half * LANES + LANES] = jnp.where(hit, 1.0, 0.0)
    line_sel_t[...] = line_sel[...].T.astype(BF16)

    def at_perforations(values):
        rows = onehot_product(line_sel[...].astype(BF16), values)
        return jnp.sum(rows * hot_x[...], axis=1, keepdims=True)

    reach_first[...] = onehot_product(line_sel_t[...], hot_dw[...] * at_perforations(low_w[...]))
    reach_last[...] = onehot_product(line_sel_t[...], hot_dw[...] * at_perforations(high_w[...]))

    pair8 = lane8 // 2
    even = lane8 % 2 == 0

    def line_ends(for_first, for_last):
        packed = jnp.zeros(piece, F32)
        for j in range(pieces):
            rows = slice(j * 8, j * 8 + 8)
            both = jnp.where(
                even,
                jnp.sum(for_last(rows), axis=1, keepdims=True),
                jnp.sum(for_first(rows), axis=1, keepdims=True),
            )
            packed = jnp.where(pair8 == j, both, packed)
        return packed

    def end_sources(values):
        return line_ends(lambda rows: low_w[rows, :] * values[rows, :], lambda rows: high_w[rows, :] * values[rows, :])

    def end_wells(seg_row):
        return line_ends(lambda rows: reach_first[rows, :] * seg_row, lambda rows: reach_last[rows, :] * seg_row)

    def send_ports(ports, packed, which):
        ports[mx] = packed + pltpu.roll(packed, LANES // 2, 1)
        fan(x_peers, ports.at[mx], ports.at[mx], which)

    def well_field(drop):
        back = jnp.sum(hot_dw[...] * drop, axis=1, keepdims=True)
        return onehot_product(line_sel_t[...], hot_x[...] * back)

    def solve_local():
        half = lines // 2
        for h in range(2):
            rows = slice(h * half, h * half + half)
            b = src[rows, :]
            for level, stride in enumerate(strides):
                t = b * recip[level, rows, :]
                b = b + low_m[level, rows, :] * pltpu.roll(t, stride, 1) + high_m[level, rows, :] * pltpu.roll(
                    t, LANES - stride, 1
                )
            src[rows, :] = b * inv[rows, :]

    def well_sums(cols):
        return jnp.sum(hot_dw[...] * cols, axis=0, keepdims=True)

    loads[4].wait()
    ends_rhs = end_sources(rhs)

    fan_wait(sw_all, ng - 1, fan_recv, 0)
    layer_all = [sum(sw_all[y * nz + g] for y in range(ny)) for g in range(nz)]
    total = sum(layer_all)
    count, bore = total[1], total[2]
    layer_sw = [layer[0] for layer in layer_all]

    def slot_of(g):
        return jnp.floor(g * count * (1.0 / nz))

    my_slot = slot_of(mz.astype(F32))
    layer_slots = [slot_of(float(g)) for g in range(nz)]
    same = [jnp.where(slot == my_slot, 1.0, 0.0) for slot in layer_slots]
    my_inv = 1.0 / (sum(m * sw for m, sw in zip(same, layer_sw)) + BORE)
    my_base = BORE * bore * my_inv
    send_ports(ports_a, ends_rhs + end_wells(my_base), 2)

    fan_wait(stat_all, nx - 1, fan_recv, 1)

    def ends_at(k):
        s, c = stat_all[k, 0], stat_all[k, 1]
        return dict(
            sz=s, sf=pltpu.roll(s, LANES - 1, 1), pz=pltpu.roll(s, LANES // 2, 1),
            pf=pltpu.roll(s, LANES // 2 - 1, 1), c=pltpu.roll(c, LANES - 1, 1),
        )

    own = ends_at(mx)

    def walk(direction):
        chain = []
        for t in range(1, nx):
            k = mx + direction * t
            valid = jnp.logical_and(k >= 0, k < nx)
            chain.append((jnp.clip(k, 0, nx - 1), valid))
        blocks = [ends_at(k) for k, _ in chain]
        ground = jnp.zeros(piece, F32)
        factors = [None] * (nx - 1)
        for t in range(nx - 1, 0, -1):
            b = blocks[t - 1]
            nearer = own if t == 1 else blocks[t - 2]
            far, near, edge = ("sf", "sz", ("pz", "pf")) if direction < 0 else ("sz", "sf", ("pf", "pz"))
            face = jnp.where(chain[t - 1][1], harmonic(b[edge[0]], nearer[edge[1]]), 0.0)
            through = b["c"] / (b["c"] + b[far] + ground)
            inner = b[near] + (b[far] + ground) * through
            outward = face / (face + inner)
            ground = inner * outward
            factors[t - 1] = (through, outward)
        reach = jnp.ones(piece, F32)
        weights = []
        for through, outward in factors:
            near_w = reach * outward
            reach = near_w * through
            weights.append((near_w, reach))
        return ground, weights, [k for k, _ in chain]

    ground_l, weights_l, index_l = walk(-1)
    ground_r, weights_r, index_r = walk(1)
    a, e, c = own["sf"] + ground_l, own["sz"] + ground_r, own["c"]
    scale = 1.0 / (a * e + (a + e) * c)
    ff, fz, zz = (e + c) * scale, c * scale, (a + c) * scale
    lower_half = lane8 < LANES // 2

    def weave(z_first, f_first, z_last, f_last):
        first = jnp.where(even, z_first, pltpu.roll(f_first, 1, 1))
        last = jnp.where(even, pltpu.roll(z_last, LANES // 2, 1), pltpu.roll(f_last, LANES // 2 + 1, 1))
        return jnp.where(lower_half, first, last)

    terms = [(mx, weave(fz, ff, zz, fz))]
    for (near_w, far_w), k in zip(weights_l, index_l):
        terms.append((k, weave(ff * near_w, ff * far_w, fz * near_w, fz * far_w)))
    for (near_w, far_w), k in zip(weights_r, index_r):
        terms.append((k, weave(fz * far_w, fz * near_w, zz * far_w, zz * near_w)))

    def end_pressures(ports):
        ends = sum(w * ports[k] for k, w in terms)
        ends = ends + pltpu.roll(ends, LANES - 1, 1)
        return [
            (lane_spread(ends, 2 * j, piece), lane_spread(ends, LANES // 2 + 2 * j, piece)) for j in range(pieces)
        ]

    def end_sums(ends):
        given = jnp.zeros(piece, F32)
        for j, (first, last) in enumerate(ends):
            rows = slice(j * 8, j * 8 + 8)
            given = given + reach_first[rows, :] * first + reach_last[rows, :] * last
        return jnp.sum(given, axis=0, keepdims=True)

    def join(ends, target):
        for j, (first, last) in enumerate(ends):
            rows = slice(j * 8, j * 8 + 8)
            target[rows, :] = src[rows, :] + low_w[rows, :] * first + high_w[rows, :] * last

    def send_row(which, row, target):
        row_send[which] = row
        fan(group_peers, row_send.at[which], target.at[mg], 3 + which)
        target[mg] = row

    src[...] = rhs[...] + well_field(my_base)
    solve_local()
    row_own = well_sums(at_perforations(src[...]))
    fan_wait(ports_a, nx - 1, fan_recv, 2)
    ends = end_pressures(ports_a)
    send_row(0, row_own + end_sums(ends), rows_a)

    join(ends, field)
    for z in range(zc):
        ysend_p[0, z] = field[z * yc : z * yc + 1, :]
        ysend_p[1, z] = field[z * yc + yc - 1 : z * yc + yc, :]
    p_halos = halos(ysend_p, yp, field, zp, 4)
    for copy in p_halos:
        copy.start()
    cols = at_perforations(field[...])
    coef_mine = [m * my_inv for m in same]
    coef_seg = []
    for g in range(nz):
        slot_sw = sum(jnp.where(layer_slots[h] == layer_slots[g], layer_sw[h], 0.0) for h in range(nz))
        coef_seg.append(1.0 / (slot_sw + BORE))
    residual_base = bore * sum(f * sw for f, sw in zip(coef_seg, layer_sw))

    for copy in p_halos:
        copy.wait_recv()
    for z in range(zc):
        rows = slice(z * yc, z * yc + yc)
        v = field[rows, :]
        below = jnp.where(row_s == 0, yp[0, z], pltpu.roll(v, 1, 0))
        above = jnp.where(row_s == yc - 1, yp[1, z], pltpu.roll(v, yc - 1, 0))
        under = field[z * yc - yc : z * yc, :] if z > 0 else zp[0]
        over = field[z * yc + yc : z * yc + 2 * yc, :] if z < zc - 1 else zp[1]
        beside = ylo[rows, :] * below + yup[rows, :] * above
        beside = beside + zface[rows, :] * under + zface[z * yc + yc : z * yc + 2 * yc, :] * over
        src[rows, :] = rhs[rows, :] + beside
    src[...] = src[...] + well_field(my_base - cols)
    ends_base = end_sources(src)

    fan_wait(rows_a, ng - 1, fan_recv, 3)
    inflow = sum(f * sum(rows_a[y * nz + g] for y in range(ny)) for g, f in enumerate(coef_mine))
    send_ports(ports_b, ends_base + end_wells(inflow), 5)
    src[...] = src[...] + well_field(inflow)
    solve_local()
    row_own = well_sums(at_perforations(src[...]))
    fan_wait(ports_b, nx - 1, fan_recv, 5)
    ends = end_pressures(ports_b)
    send_row(1, row_own + end_sums(ends), rows_b)
    join(ends, p_out)
    fan_wait(rows_b, ng - 1, fan_recv, 4)
    res = sum(f * sum(rows_b[y * nz + g] for y in range(ny)) for g, f in enumerate(coef_seg)) - residual_base
    res_out[...] = pltpu.roll(res, lax.rem(LANES - mg * wells, LANES), 1)[:, :wells]

    for copy in perm_halos + p_halos:
        copy.wait_send()
    fan_wait(sw_all, ng - 1, fan_send, 0)
    fan_wait(stat_all, nx - 1, fan_send, 1)
    fan_wait(ports_a, nx - 1, fan_send, 2)
    fan_wait(rows_a, ng - 1, fan_send, 3)
    fan_wait(rows_b, ng - 1, fan_send, 4)
    fan_wait(ports_b, nx - 1, fan_send, 5)


def shards(dims, rhs, perm_x, perm_y, perm_z, storage, perf_cell, perf_well, perf_index, seg_count, bhp):
    nx, ny, nz, zc, yc, wells = dims
    ng = ny * nz
    lines = zc * yc
    perfs = ng * 8
    plane = (lines, LANES)
    flat = [a.reshape(plane) for a in (rhs, perm_x, perm_y, perm_z, storage)]
    slots = [a[0, 0].T for a in (perf_cell, perf_well, perf_index)]
    operands = [pltpu.with_memory_space_constraint(a, pltpu.HBM) for a in (*slots, seg_count[0], bhp[0], *flat)]
    vmem = pl.BlockSpec(memory_space=pltpu.VMEM)
    hbm = pl.BlockSpec(memory_space=pltpu.HBM)
    whole = pltpu.VMEM(plane, F32)
    perf_plane = pltpu.VMEM((perfs, LANES), F32)
    pressure, residual = pl.pallas_call(
        functools.partial(kernel, dims),
        out_shape=(pltpu.VMEM(plane, F32), pltpu.VMEM((1, wells), F32)),
        in_specs=[hbm] * 10,
        out_specs=(vmem, vmem),
        scratch_shapes=[pltpu.VMEM((8, ng), jnp.int32)] * 2
        + [pltpu.VMEM((8, ng), F32), pltpu.SMEM((1, wells), jnp.int32), pltpu.SMEM((1, wells), F32)]
        + [whole] * 5
        + [whole] * 5
        + [pltpu.VMEM((lines + yc, LANES), F32)]
        + [pltpu.VMEM((7, lines, LANES), F32)] * 3
        + [whole] * 5
        + [perf_plane] * 2
        + [pltpu.VMEM((perfs, lines), F32), pltpu.VMEM((lines, perfs), BF16)]
        + [whole] * 2
        + [pltpu.VMEM((2, zc, 1, LANES), F32), pltpu.VMEM((2, yc, LANES), F32)]
        + [pltpu.VMEM((2, zc, 1, LANES), F32)] * 3
        + [pltpu.VMEM((2, yc, LANES), F32)]
        + [pltpu.VMEM((3, 1, LANES), F32), pltpu.VMEM((ng, 3, 1, LANES), F32)]
        + [pltpu.VMEM((2, 1, LANES), F32)]
        + [pltpu.VMEM((ng, 1, LANES), F32)] * 2
        + [pltpu.VMEM((nx, 2, 8, LANES), F32)]
        + [pltpu.VMEM((nx, 8, LANES), F32)] * 2
        + [
            pltpu.SemaphoreType.DMA((10,)),
            pltpu.SemaphoreType.DMA((8,)),
            pltpu.SemaphoreType.DMA((8,)),
            pltpu.SemaphoreType.DMA((6,)),
            pltpu.SemaphoreType.DMA((6,)),
        ],
        compiler_params=pltpu.CompilerParams(
            collective_id=0, has_side_effects=True, vmem_limit_bytes=32 * 1024 * 1024
        ),
        name="sweeps",
    )(*operands)
    return pressure.reshape(rhs.shape), residual.reshape(1, 1, wells)


def solution(mesh):
    nx, ny, nz = mesh.shape["gx"], mesh.shape["gy"], mesh.shape["gz"]
    cells = P("gz", "gy", "gx")
    perfs = P("gx", ("gy", "gz"), None, None)
    owned = P("gx", ("gy", "gz"), None)

    def program(rhs, perm_x, perm_y, perm_z, storage, perf_cell, perf_well, perf_index, seg_count, bhp):
        dims = (nx, ny, nz, rhs.shape[0] // nz, rhs.shape[1] // ny, seg_count.shape[-1])
        return jax.shard_map(
            functools.partial(shards, dims),
            mesh=mesh,
            in_specs=(cells,) * 5 + (perfs,) * 3 + (owned,) * 2,
            out_specs=(cells, owned),
            check_vma=False,
        )(rhs, perm_x, perm_y, perm_z, storage, perf_cell, perf_well, perf_index, seg_count, bhp)

    return program
```

time: 41.4 us -> 38.6 us (0.932)
  Pallas kernels: 39.5 us -> 36.7 us
    pallas_call x1, Pallas kernels: 39.5 us -> 36.7 us  [shards(): pl.pallas_call(functools.partial(kernel, dims), out_shape=(pltpu.VMEM(pla...]
where the time goes in v3:
time: 38.6 us; the launch traced here: 38.5 us
  Pallas kernels  36.7 us (95%)
  local copies, waits for them, and re-layouts  1.17 us (3%)
  between operations  0.64 us (2%)
    pallas_call x1, Pallas kernels, shards(): pl.pallas_call(functools.partial(kernel, dims), out_shape=(pltpu.VMEM(pla...  36.7 us
    unnamed x2, local copies, waits for them, and re-layouts  1.17 us

profile of v3, /device:TPU:1, one launch (start us, length us, event | category | flops | bytes accessed | tf_op | source)
XLA Modules:
  0.0 38.5 jit_solution(10295338650050635125)
XLA Ops:
  0.6 36.7 %sweeps.1 = (f32[256,128]{1,0:T(8,128)S(1)}, f32[1,4]{1,0:T(1,128)S(1)}) custom-call(s32[8,32]{1,0:T(8,128)} %bitcast.25, s32[8,32]{1,0:T(8,128)} %bitcast.26, f32[8,32]{1,0:T(8,128)} %bitcast.27, s32[1,4]{1,0:T(1,128)} %bitcast.28, f32[1,4]{1,0:T(1,128)} %bitcast.29, f32[256,128]{1,0:T(8,128)} %bitcast.20, f32[256,128]{1,0:T(8,128)} %bitcast.21, ...), custom_call_target="tpu_custom_call" | custom-call | tf_op jit(solution)/shard_map/sweeps/pallas_call | solution.py:461
  37.3 0.7 %copy.14 = f32[8,32,128]{2,1,0:T(8,128)} copy(f32[8,32,128]{2,1,0:T(8,128)S(1)} %bitcast.18) | data formatting | bytes 262144
  38.0 0.5 %copy.15 = f32[1,1,4]{2,1,0:T(1,128)} copy(f32[1,1,4]{2,1,0:T(1,128)S(1)} %bitcast.19) | data formatting | bytes 32

commit v4 on v3

--- a/solution.py
+++ b/solution.py
@@ -158,6 +158,15 @@
     fan(group_peers, sw_send, sw_all.at[mg], 0)
     sw_all[mg] = sw_send[...]
 
+    for d in range(ng):
+        c = lane_spread(code, d, piece)
+        rows = slice(d * 8, d * 8 + 8)
+        hot_x[rows, :] = jnp.where(lane8 == jnp.bitwise_and(c, LANES - 1), 1.0, 0.0)
+        for half in range(lines // LANES):
+            hit = lane8 == jnp.right_shift(c, 7) - half * LANES
+            line_sel[rows, half * LANES : half * LANES + LANES] = jnp.where(hit, 1.0, 0.0)
+    line_sel_t[...] = line_sel[...].T.astype(BF16)
+
     loads[2].wait()
     loads[3].wait()
     lane_s = lane_of((yc, LANES))
@@ -173,6 +182,54 @@
         ylo[rows, :] = f
         if z > 0:
             zface[rows, :] = harmonic(pz[z * yc - yc : z * yc, :], pz[rows, :])
+    strides = [1 << i for i in range(7)]
+
+    def reduce_matrix(groups):
+        for slices in groups:
+            lo, hi, s = [jnp.concatenate([ref[rows, :] for rows in slices], axis=0) for ref in (left, right, sig)]
+            lane_c = lane_of(lo.shape)
+
+            def keep(ref, value, *at):
+                start = 0
+                for rows in slices:
+                    size = rows.stop - rows.start
+                    ref[(*at, rows, slice(None))] = value[start : start + size]
+                    start += size
+
+            for level, stride in enumerate(strides):
+                r = 1.0 / (s + lo + hi)
+                from_low = lane_c > stride
+                from_high = lane_c < LANES - 1 - stride
+                a = jnp.where(from_low, lo, 0.0)
+                g = jnp.where(from_high, hi, 0.0)
+                keep(low_m, a, level)
+                keep(high_m, g, level)
+                keep(recip, r, level)
+                q = s * r
+                s = s + a * pltpu.roll(q, stride, 1) + g * pltpu.roll(q, LANES - stride, 1)
+                lo = jnp.where(from_low, lo * pltpu.roll(lo * r, stride, 1), lo)
+                hi = jnp.where(from_high, hi * pltpu.roll(hi * r, LANES - stride, 1), hi)
+            r = 1.0 / (s + lo + hi)
+            first, last = lane_c == 0, lane_c == LANES - 1
+            keep(inv, jnp.where(jnp.logical_or(first, last), 0.0, r))
+            keep(low_w, jnp.where(first, 1.0, jnp.where(last, 0.0, lo * r)))
+            keep(high_w, jnp.where(last, 1.0, jnp.where(first, 0.0, hi * r)))
+            keep(sig, s)
+            keep(right, hi)
+
+    tile = 8
+    inner = [[slice(z * yc + tile, z * yc + yc - tile) for z in range(1, zc - 1)]]
+    edge = [slice(z * yc + o, z * yc + o + tile) for z in range(1, zc - 1) for o in (0, yc - tile)]
+    cut = len(edge) // 2
+    outer = [[slice(0, yc)] + edge[:cut], [slice(lines - yc, lines)] + edge[cut:]]
+    for slices in inner:
+        for rows in slices:
+            sig[rows, :] = (
+                st[rows, :] + ylo[rows, :] + ylo[rows.start + 1 : rows.stop + 1, :]
+                + zface[rows, :] + zface[rows.start + yc : rows.stop + yc, :]
+            )
+    reduce_matrix(inner)
+
     for copy in perm_halos:
         copy.wait_recv()
     zface[0:yc, :] = jnp.where(mz == 0, 0.0, harmonic(zperm[0], pz[0:yc, :]))
@@ -185,38 +242,14 @@
         g = jnp.where(row_s == yc - 1, top, pltpu.roll(f, yc - 1, 0))
         ylo[rows, :] = f
         yup[rows, :] = g
-        sig[rows, :] = st[rows, :] + f + g + zface[rows, :] + zface[z * yc + yc : z * yc + 2 * yc, :]
-
-    chunk = 128
-    lane_c = lane_of((chunk, LANES))
-    strides = [1 << i for i in range(7)]
-
-    def reduce_matrix(i, carry):
-        rows = pl.ds(pl.multiple_of(i * chunk, chunk), chunk)
-        lo, hi, s = left[rows, :], right[rows, :], sig[rows, :]
-        for level, stride in enumerate(strides):
-            r = 1.0 / (s + lo + hi)
-            from_low = lane_c > stride
-            from_high = lane_c < LANES - 1 - stride
-            a = jnp.where(from_low, lo, 0.0)
-            g = jnp.where(from_high, hi, 0.0)
-            low_m[level, rows, :] = a
-            high_m[level, rows, :] = g
-            recip[level, rows, :] = r
-            q = s * r
-            s = s + a * pltpu.roll(q, stride, 1) + g * pltpu.roll(q, LANES - stride, 1)
-            lo = jnp.where(from_low, lo * pltpu.roll(lo * r, stride, 1), lo)
-            hi = jnp.where(from_high, hi * pltpu.roll(hi * r, LANES - stride, 1), hi)
-        r = 1.0 / (s + lo + hi)
-        first, last = lane_c == 0, lane_c == LANES - 1
-        inv[rows, :] = jnp.where(jnp.logical_or(first, last), 0.0, r)
-        low_w[rows, :] = jnp.where(first, 1.0, jnp.where(last, 0.0, lo * r))
-        high_w[rows, :] = jnp.where(last, 1.0, jnp.where(first, 0.0, hi * r))
-        sig[rows, :] = s
-        right[rows, :] = hi
-        return carry
-
-    lax.fori_loop(0, lines // chunk, reduce_matrix, 0)
+        total = st[rows, :] + f + g + zface[rows, :] + zface[z * yc + yc : z * yc + 2 * yc, :]
+        if z in (0, zc - 1):
+            sig[rows, :] = total
+        else:
+            for o in (0, yc - tile):
+                sig[z * yc + o : z * yc + o + tile, :] = total[o : o + tile]
+
+    reduce_matrix(outer)
 
     def ends_of(ref):
         return pack_ends([ref[j * 8 : j * 8 + 8, :] for j in range(pieces)])
@@ -224,15 +257,6 @@
     stat_all[mx, 0] = ends_of(sig) + pltpu.roll(ends_of(px), LANES // 2, 1)
     stat_all[mx, 1] = ends_of(right)
     fan(x_peers, stat_all.at[mx], stat_all.at[mx], 1)
-
-    for d in range(ng):
-        c = lane_spread(code, d, piece)
-        rows = slice(d * 8, d * 8 + 8)
-        hot_x[rows, :] = jnp.where(lane8 == jnp.bitwise_and(c, LANES - 1), 1.0, 0.0)
-        for half in range(lines // LANES):
-            hit = lane8 == jnp.right_shift(c, 7) - half * LANES
-            line_sel[rows, half * LANES : half * LANES + LANES] = jnp.where(hit, 1.0, 0.0)
-    line_sel_t[...] = line_sel[...].T.astype(BF16)
 
     def at_perforations(values):
         rows = onehot_product(line_sel[...].astype(BF16), values)
@@ -303,6 +327,10 @@
     my_inv = 1.0 / (sum(m * sw for m, sw in zip(same, layer_sw)) + BORE)
     my_base = BORE * bore * my_inv
     send_ports(ports_a, ends_rhs + end_wells(my_base), 2)
+
+    src[...] = rhs[...] + well_field(my_base)
+    solve_local()
+    row_own = well_sums(at_perforations(src[...]))
 
     fan_wait(stat_all, nx - 1, fan_recv, 1)
 
@@ -329,17 +357,17 @@
             nearer = own if t == 1 else blocks[t - 2]
             far, near, edge = ("sf", "sz", ("pz", "pf")) if direction < 0 else ("sz", "sf", ("pf", "pz"))
             face = jnp.where(chain[t - 1][1], harmonic(b[edge[0]], nearer[edge[1]]), 0.0)
-            through = b["c"] / (b["c"] + b[far] + ground)
-            inner = b[near] + (b[far] + ground) * through
-            outward = face / (face + inner)
-            ground = inner * outward
-            factors[t - 1] = (through, outward)
+            shunt = b[far] + ground
+            joined = b["c"] + shunt
+            inner = b[near] * joined + shunt * b["c"]
+            part = face / (face * joined + inner)
+            ground = inner * part
+            factors[t - 1] = (part * joined, part * b["c"])
         reach = jnp.ones(piece, F32)
         weights = []
-        for through, outward in factors:
-            near_w = reach * outward
-            reach = near_w * through
-            weights.append((near_w, reach))
+        for from_near, from_far in factors:
+            weights.append((reach * from_near, reach * from_far))
+            reach = weights[-1][1]
         return ground, weights, [k for k, _ in chain]
 
     ground_l, weights_l, index_l = walk(-1)
@@ -384,9 +412,6 @@
         fan(group_peers, row_send.at[which], target.at[mg], 3 + which)
         target[mg] = row
 
-    src[...] = rhs[...] + well_field(my_base)
-    solve_local()
-    row_own = well_sums(at_perforations(src[...]))
     fan_wait(ports_a, nx - 1, fan_recv, 2)
     ends = end_pressures(ports_a)
     send_row(0, row_own + end_sums(ends), rows_a)

time: 38.6 us -> 37.6 us (0.974)
  Pallas kernels: 36.7 us -> 35.7 us
    pallas_call x1, Pallas kernels: 36.7 us -> 35.7 us  [shards(): pl.pallas_call(functools.partial(kernel, dims), out_shape=(pltpu.VMEM(pla...]
where the time goes in v4:
time: 37.6 us; the launch traced here: 37.5 us
  Pallas kernels  35.7 us (95%)
  local copies, waits for them, and re-layouts  1.17 us (3%)
  between operations  0.64 us (2%)
    pallas_call x1, Pallas kernels, shards(): pl.pallas_call(functools.partial(kernel, dims), out_shape=(pltpu.VMEM(pla...  35.7 us
    unnamed x2, local copies, waits for them, and re-layouts  1.17 us

profile of v4, /device:TPU:1, one launch (start us, length us, event | category | flops | bytes accessed | tf_op | source)
XLA Modules:
  0.0 37.5 jit_solution(13483378279836048146)
XLA Ops:
  0.6 35.7 %sweeps.1 = (f32[256,128]{1,0:T(8,128)S(1)}, f32[1,4]{1,0:T(1,128)S(1)}) custom-call(s32[8,32]{1,0:T(8,128)} %bitcast.25, s32[8,32]{1,0:T(8,128)} %bitcast.26, f32[8,32]{1,0:T(8,128)} %bitcast.27, s32[1,4]{1,0:T(1,128)} %bitcast.28, f32[1,4]{1,0:T(1,128)} %bitcast.29, f32[256,128]{1,0:T(8,128)} %bitcast.20, f32[256,128]{1,0:T(8,128)} %bitcast.21, ...), custom_call_target="tpu_custom_call" | custom-call | tf_op jit(solution)/shard_map/sweeps/pallas_call | solution.py:486
  36.4 0.7 %copy.14 = f32[8,32,128]{2,1,0:T(8,128)} copy(f32[8,32,128]{2,1,0:T(8,128)S(1)} %bitcast.18) | data formatting | bytes 262144
  37.0 0.5 %copy.15 = f32[1,1,4]{2,1,0:T(1,128)} copy(f32[1,1,4]{2,1,0:T(1,128)S(1)} %bitcast.19) | data formatting | bytes 32

commit v5 on v4

--- a/solution.py
+++ b/solution.py
@@ -295,9 +295,10 @@
         return onehot_product(line_sel_t[...], hot_x[...] * back)
 
     def solve_local():
-        half = lines // 2
-        for h in range(2):
-            rows = slice(h * half, h * half + half)
+        size = 128
+
+        def part(i, carry):
+            rows = pl.ds(pl.multiple_of(i * size, size), size)
             b = src[rows, :]
             for level, stride in enumerate(strides):
                 t = b * recip[level, rows, :]
@@ -305,6 +306,9 @@
                     t, LANES - stride, 1
                 )
             src[rows, :] = b * inv[rows, :]
+            return carry
+
+        lax.fori_loop(0, lines // size, part, 0)
 
     def well_sums(cols):
         return jnp.sum(hot_dw[...] * cols, axis=0, keepdims=True)

time: 37.6 us -> 37.1 us (0.987)
  Pallas kernels: 35.7 us -> 35.1 us
    pallas_call x1, Pallas kernels: 35.7 us -> 35.1 us  [shards(): pl.pallas_call(functools.partial(kernel, dims), out_shape=(pltpu.VMEM(pla...]
where the time goes in v5:
time: 37.1 us; the launch traced here: 37 us
  Pallas kernels  35.1 us (95%)
  local copies, waits for them, and re-layouts  1.17 us (3%)
  between operations  0.64 us (2%)
    pallas_call x1, Pallas kernels, shards(): pl.pallas_call(functools.partial(kernel, dims), out_shape=(pltpu.VMEM(pla...  35.1 us
    unnamed x2, local copies, waits for them, and re-layouts  1.17 us

profile of v5, /device:TPU:1, one launch (start us, length us, event | category | flops | bytes accessed | tf_op | source)
XLA Modules:
  0.0 37.0 jit_solution(12648576096944773005)
XLA Ops:
  0.6 35.1 %sweeps.1 = (f32[256,128]{1,0:T(8,128)S(1)}, f32[1,4]{1,0:T(1,128)S(1)}) custom-call(s32[8,32]{1,0:T(8,128)} %bitcast.25, s32[8,32]{1,0:T(8,128)} %bitcast.26, f32[8,32]{1,0:T(8,128)} %bitcast.27, s32[1,4]{1,0:T(1,128)} %bitcast.28, f32[1,4]{1,0:T(1,128)} %bitcast.29, f32[256,128]{1,0:T(8,128)} %bitcast.20, f32[256,128]{1,0:T(8,128)} %bitcast.21, ...), custom_call_target="tpu_custom_call" | custom-call | tf_op jit(solution)/shard_map/sweeps/pallas_call | solution.py:490
  35.8 0.7 %copy.14 = f32[8,32,128]{2,1,0:T(8,128)} copy(f32[8,32,128]{2,1,0:T(8,128)S(1)} %bitcast.18) | data formatting | bytes 262144
  36.4 0.5 %copy.15 = f32[1,1,4]{2,1,0:T(1,128)} copy(f32[1,1,4]{2,1,0:T(1,128)S(1)} %bitcast.19) | data formatting | bytes 32

commit v6 on v5

--- a/solution.py
+++ b/solution.py
@@ -42,6 +42,14 @@
     return jnp.broadcast_to(x[:, lane : lane + 1], shape)
 
 
+def tree_sum(values):
+    values = list(values)
+    while len(values) > 1:
+        pairs = [a + b for a, b in zip(values[::2], values[1::2])]
+        values = pairs + values[len(pairs) * 2 :]
+    return values[0]
+
+
 def pack_ends(pieces):
     pair = lane_of((8, LANES)) // 2
     packed = jnp.zeros((8, LANES), F32)
@@ -54,7 +62,7 @@
     dims, cell_in, well_in, wgt_in, cnt_in, bhp_in, rhs_in, px_in, py_in, pz_in, st_in, p_out, res_out,
     cell_ref, well_ref, wgt_ref, cnt_ref, bhp_ref, rhs, px, py, pz, st,
     sig, left, right, ylo, yup, zface, low_m, high_m, recip, inv, low_w, high_w, src, field,
-    hot_x, hot_dw, line_sel, line_sel_t, reach_first, reach_last,
+    hot_x, hot_dw, line_sel, line_sel_b, line_sel_t, reach_first, reach_last,
     yperm, zperm, yp, ysend_perm, ysend_p, zp,
     sw_send, sw_all, row_send, rows_a, rows_b, stat_all, ports_a, ports_b,
     in_sem, halo_send, halo_recv, fan_send, fan_recv,
@@ -165,6 +173,7 @@
         for half in range(lines // LANES):
             hit = lane8 == jnp.right_shift(c, 7) - half * LANES
             line_sel[rows, half * LANES : half * LANES + LANES] = jnp.where(hit, 1.0, 0.0)
+    line_sel_b[...] = line_sel[...].astype(BF16)
     line_sel_t[...] = line_sel[...].T.astype(BF16)
 
     loads[2].wait()
@@ -259,7 +268,7 @@
     fan(x_peers, stat_all.at[mx], stat_all.at[mx], 1)
 
     def at_perforations(values):
-        rows = onehot_product(line_sel[...].astype(BF16), values)
+        rows = onehot_product(line_sel_b[...], values)
         return jnp.sum(rows * hot_x[...], axis=1, keepdims=True)
 
     reach_first[...] = onehot_product(line_sel_t[...], hot_dw[...] * at_perforations(low_w[...]))
@@ -269,7 +278,7 @@
     even = lane8 % 2 == 0
 
     def line_ends(for_first, for_last):
-        packed = jnp.zeros(piece, F32)
+        packed = [jnp.zeros(piece, F32)] * 4
         for j in range(pieces):
             rows = slice(j * 8, j * 8 + 8)
             both = jnp.where(
@@ -277,8 +286,8 @@
                 jnp.sum(for_last(rows), axis=1, keepdims=True),
                 jnp.sum(for_first(rows), axis=1, keepdims=True),
             )
-            packed = jnp.where(pair8 == j, both, packed)
-        return packed
+            packed[j % 4] = jnp.where(pair8 == j, both, packed[j % 4])
+        return tree_sum(packed)
 
     def end_sources(values):
         return line_ends(lambda rows: low_w[rows, :] * values[rows, :], lambda rows: high_w[rows, :] * values[rows, :])
@@ -317,8 +326,8 @@
     ends_rhs = end_sources(rhs)
 
     fan_wait(sw_all, ng - 1, fan_recv, 0)
-    layer_all = [sum(sw_all[y * nz + g] for y in range(ny)) for g in range(nz)]
-    total = sum(layer_all)
+    layer_all = [tree_sum(sw_all[y * nz + g] for y in range(ny)) for g in range(nz)]
+    total = tree_sum(layer_all)
     count, bore = total[1], total[2]
     layer_sw = [layer[0] for layer in layer_all]
 
@@ -393,18 +402,18 @@
         terms.append((k, weave(fz * far_w, fz * near_w, zz * far_w, zz * near_w)))
 
     def end_pressures(ports):
-        ends = sum(w * ports[k] for k, w in terms)
+        ends = tree_sum(w * ports[k] for k, w in terms)
         ends = ends + pltpu.roll(ends, LANES - 1, 1)
         return [
             (lane_spread(ends, 2 * j, piece), lane_spread(ends, LANES // 2 + 2 * j, piece)) for j in range(pieces)
         ]
 
     def end_sums(ends):
-        given = jnp.zeros(piece, F32)
+        lanes = [0.0] * 8
         for j, (first, last) in enumerate(ends):
             rows = slice(j * 8, j * 8 + 8)
-            given = given + reach_first[rows, :] * first + reach_last[rows, :] * last
-        return jnp.sum(given, axis=0, keepdims=True)
+            lanes[j % 8] = lanes[j % 8] + (reach_first[rows, :] * first + reach_last[rows, :] * last)
+        return jnp.sum(tree_sum(lanes), axis=0, keepdims=True)
 
     def join(ends, target):
         for j, (first, last) in enumerate(ends):
@@ -451,7 +460,7 @@
     ends_base = end_sources(src)
 
     fan_wait(rows_a, ng - 1, fan_recv, 3)
-    inflow = sum(f * sum(rows_a[y * nz + g] for y in range(ny)) for g, f in enumerate(coef_mine))
+    inflow = tree_sum(f * tree_sum(rows_a[y * nz + g] for y in range(ny)) for g, f in enumerate(coef_mine))
     send_ports(ports_b, ends_base + end_wells(inflow), 5)
     src[...] = src[...] + well_field(inflow)
     solve_local()
@@ -461,7 +470,7 @@
     send_row(1, row_own + end_sums(ends), rows_b)
     join(ends, p_out)
     fan_wait(rows_b, ng - 1, fan_recv, 4)
-    res = sum(f * sum(rows_b[y * nz + g] for y in range(ny)) for g, f in enumerate(coef_seg)) - residual_base
+    res = tree_sum(f * tree_sum(rows_b[y * nz + g] for y in range(ny)) for g, f in enumerate(coef_seg)) - residual_base
     res_out[...] = pltpu.roll(res, lax.rem(LANES - mg * wells, LANES), 1)[:, :wells]
 
     for copy in perm_halos + p_halos:
@@ -500,7 +509,7 @@
         + [pltpu.VMEM((7, lines, LANES), F32)] * 3
         + [whole] * 5
         + [perf_plane] * 2
-        + [pltpu.VMEM((perfs, lines), F32), pltpu.VMEM((lines, perfs), BF16)]
+        + [pltpu.VMEM((perfs, lines), F32), pltpu.VMEM((perfs, lines), BF16), pltpu.VMEM((lines, perfs), BF16)]
         + [whole] * 2
         + [pltpu.VMEM((2, zc, 1, LANES), F32), pltpu.VMEM((2, yc, LANES), F32)]
         + [pltpu.VMEM((2, zc, 1, LANES), F32)] * 3

time: 37.1 us -> 37.1 us (level)
  no operation moved by 1% of the time
where the time goes in v6:
time: 37.1 us; the launch traced here: 37 us
  Pallas kernels  35.1 us (95%)
  local copies, waits for them, and re-layouts  1.17 us (3%)
  between operations  0.64 us (2%)
    pallas_call x1, Pallas kernels, shards(): pl.pallas_call(functools.partial(kernel, dims), out_shape=(pltpu.VMEM(pla...  35.1 us
    unnamed x2, local copies, waits for them, and re-layouts  1.17 us

profile of v6, /device:TPU:1, one launch (start us, length us, event | category | flops | bytes accessed | tf_op | source)
XLA Modules:
  0.0 37.0 jit_solution(2007721322539025335)
XLA Ops:
  0.6 35.1 %sweeps.1 = (f32[256,128]{1,0:T(8,128)S(1)}, f32[1,4]{1,0:T(1,128)S(1)}) custom-call(s32[8,32]{1,0:T(8,128)} %bitcast.25, s32[8,32]{1,0:T(8,128)} %bitcast.26, f32[8,32]{1,0:T(8,128)} %bitcast.27, s32[1,4]{1,0:T(1,128)} %bitcast.28, f32[1,4]{1,0:T(1,128)} %bitcast.29, f32[256,128]{1,0:T(8,128)} %bitcast.20, f32[256,128]{1,0:T(8,128)} %bitcast.21, ...), custom_call_target="tpu_custom_call" | custom-call | tf_op jit(solution)/shard_map/sweeps/pallas_call | solution.py:499
  35.8 0.7 %copy.14 = f32[8,32,128]{2,1,0:T(8,128)} copy(f32[8,32,128]{2,1,0:T(8,128)S(1)} %bitcast.18) | data formatting | bytes 262144
  36.4 0.5 %copy.15 = f32[1,1,4]{2,1,0:T(1,128)} copy(f32[1,1,4]{2,1,0:T(1,128)S(1)} %bitcast.19) | data formatting | bytes 32
